TPU v7x, 32 devices: a whole 2x2x4 slice. The times are simulated.
32 devices in a mesh: qubit: 16 (over z, x, core), head: 2 (over y).
Axes of the slice: x: 2, y: 2, z: 4, core: 2. Of those that a mesh axis runs over, the one named last changes fastest.
Arguments:
- tokens: bfloat16 [128, 256, 512], P('qubit'), may hold values from -6 to 6
- kv_cache: bfloat16 [128, 8, 384, 128], P('qubit', 'head'), may hold values from -6 to 6
- cache_age: int32 [128, 3], P('qubit'), may hold values from 1 to 8
- partner: int32 [128], P('qubit'), may hold values from 0 to 127, as said below
- slope: float32 [8], P('head'), may hold values from 0.03 to 1.5
- w_qkv: bfloat16 [3, 512, 512], P(None, None, 'head'), may hold values from -0.25 to 0.25
- w_o: bfloat16 [512, 512], replicated, may hold values from -0.25 to 0.25
- attn_gain: float32 [512], replicated, may hold values from 0.5 to 1.5
- mlp_gain: float32 [512], replicated, may hold values from 0.5 to 1.5
- w_in: bfloat16 [512, 2048], P(None, 'head'), may hold values from -0.25 to 0.25
- w_down: bfloat16 [2048, 512], P('head'), may hold values from -0.125 to 0.125
Outputs:
- decoded: bfloat16 [128, 256, 512], P('qubit', 'head')
Inputs may be any that keep to these rules, and one draw needn't show every extreme that they name: partner pairs the qubits: partner[partner[q]] = q. With H = 8, the 8 qubits of device d (q // 8 = d) carry the colours 0 to 7, one each, in an order drawn per device; the qubit of colour c pairs with the qubit of colour c on device H + (d + c) mod H if d < H, on device (d - H - c) mod H if d >= H.
All inputs are finite; a program needn't handle non-finite values.
Results may differ from a plain program's by a relative error of at most 0.0065.
Values may be sent and summed in bfloat16 or wider, within the bound.
A program may use at most 128 MiB of HBM per device.

v0:
```python
import jax
import jax.numpy as jnp
from jax import lax
from jax.sharding import PartitionSpec as P

DH = 64
STAB = 128


def rms_scale(values, gain):
    return values * lax.rsqrt(jnp.mean(values * values, axis=-1, keepdims=True) + 1e-06) * gain


def cache_bias(age_row, slope, new_len):
    key_age = jnp.repeat(age_row.astype(jnp.float32), STAB)
    query_round = (jnp.arange(new_len) // STAB).astype(jnp.float32)
    return -slope[:, None, None] * (key_age[None, None, :] + query_round[None, :, None])


def fresh_bias(slope, new_len):
    round_idx = jnp.arange(new_len) // STAB
    allowed = round_idx[None, :] <= round_idx[:, None]
    distance = (round_idx[:, None] - round_idx[None, :]).astype(jnp.float32)
    return jnp.where(allowed[None], -slope[:, None, None] * distance[None], -1e30)


def block_partial(queries, key_set, value_set, bias):
    logits = (
        jnp.einsum("thd,hkd->htk", queries, key_set, preferred_element_type=jnp.float32)
        * DH ** (-0.5)
        + bias
    )
    top = jnp.max(logits, axis=-1)
    weights = jnp.exp(logits - top[..., None])
    summed = jnp.einsum(
        "htk,hkd->htd", weights.astype(jnp.bfloat16), value_set, preferred_element_type=jnp.float32
    )
    return (top, jnp.sum(weights, axis=-1), summed)


def on_device(
    tokens, kv_cache, cache_age, partner, slope, w_qkv, w_o, attn_gain, mlp_gain, w_in, w_down
):
    local_count = tokens.shape[0]
    new_len = tokens.shape[1]
    width = tokens.shape[2]
    heads_here = slope.shape[0]
    qubit_devs = lax.axis_size("qubit")
    widened = tokens.astype(jnp.float32)
    normed = rms_scale(widened, attn_gain).astype(jnp.bfloat16)
    queries = (
        jnp.dot(normed, w_qkv[0], preferred_element_type=jnp.float32)
        .astype(jnp.bfloat16)
        .reshape(local_count, new_len, heads_here, DH)
    )
    fresh_k = (
        jnp.dot(normed, w_qkv[1], preferred_element_type=jnp.float32)
        .astype(jnp.bfloat16)
        .reshape(local_count, new_len, heads_here, DH)
    )
    fresh_v = (
        jnp.dot(normed, w_qkv[2], preferred_element_type=jnp.float32)
        .astype(jnp.bfloat16)
        .reshape(local_count, new_len, heads_here, DH)
    )
    owner_dev = partner // local_count
    pick_rows = owner_dev[None, :] == jnp.arange(qubit_devs, dtype=jnp.int32)[:, None]
    recent_bias = fresh_bias(slope, new_len)

    def own_partial(entry):
        query_block, cache_block, age_row, key_block, value_block = entry
        key_set = jnp.concatenate(
            [cache_block[..., :DH], jnp.transpose(key_block, (1, 0, 2))], axis=1
        )
        value_set = jnp.concatenate(
            [cache_block[..., DH:], jnp.transpose(value_block, (1, 0, 2))], axis=1
        )
        bias = jnp.concatenate([cache_bias(age_row, slope, new_len), recent_bias], axis=2)
        return block_partial(query_block, key_set, value_set, bias)

    near_part = lax.map(own_partial, (queries, kv_cache, cache_age, fresh_k, fresh_v))

    def mate_partial(entry):
        query_block, cache_block, age_row = entry
        return block_partial(
            query_block,
            cache_block[..., :DH],
            cache_block[..., DH:],
            cache_bias(age_row, slope, new_len),
        )

    send_cache = jnp.einsum(
        "ej,jhkc->ehkc",
        pick_rows.astype(jnp.bfloat16),
        kv_cache,
        preferred_element_type=jnp.float32,
    ).astype(jnp.bfloat16)
    send_age = jnp.sum(pick_rows.astype(jnp.int32)[:, :, None] * cache_age[None], axis=1)
    got_cache, got_age = (
        lax.all_to_all(send_cache, "qubit", split_axis=0, concat_axis=0, tiled=True),
        lax.all_to_all(send_age, "qubit", split_axis=0, concat_axis=0, tiled=True),
    )
    mate_cache = jnp.take(got_cache, owner_dev, axis=0)
    mate_age = jnp.take(got_age, owner_dev, axis=0)
    far_part = lax.map(mate_partial, (queries, mate_cache, mate_age))
    joint_top = jnp.maximum(near_part[0], far_part[0])
    near_factor = jnp.exp(near_part[0] - joint_top)
    far_factor = jnp.exp(far_part[0] - joint_top)
    joint_total = near_part[1] * near_factor + far_part[1] * far_factor
    joint_sum = near_part[2] * near_factor[..., None] + far_part[2] * far_factor[..., None]
    attended = joint_sum / joint_total[..., None]
    attended = (
        jnp.transpose(attended, (0, 2, 1, 3))
        .reshape(local_count, new_len, heads_here * DH)
        .astype(jnp.bfloat16)
    )
    regrouped = lax.all_to_all(attended, "head", split_axis=1, concat_axis=2, tiled=True)
    tok_rows = regrouped.shape[1]
    head_pos = lax.axis_index("head")
    residual_in = lax.dynamic_slice_in_dim(widened, head_pos * tok_rows, tok_rows, 1)
    hidden_state = residual_in + jnp.dot(regrouped, w_o, preferred_element_type=jnp.float32)
    normed_local = (
        rms_scale(hidden_state, mlp_gain)
        .astype(jnp.bfloat16)
        .reshape(local_count * tok_rows, width)
    )
    activated = jax.nn.gelu(
        jnp.dot(
            normed_local,
            lax.all_gather(w_in, "head", axis=1, tiled=True),
            preferred_element_type=jnp.float32,
        )
    ).astype(jnp.bfloat16)
    mlp_sum = jnp.dot(
        activated,
        lax.all_gather(w_down, "head", axis=0, tiled=True),
        preferred_element_type=jnp.float32,
    )
    return (hidden_state + mlp_sum.reshape(local_count, tok_rows, width)).astype(jnp.bfloat16)


def solution(mesh):
    in_specs = (
        P("qubit", None, None),
        P("qubit", "head", None, None),
        P("qubit", None),
        P("qubit"),
        P("head"),
        P(None, None, "head"),
        P(),
        P(),
        P(),
        P(None, "head"),
        P("head", None),
    )
    out_specs = P("qubit", "head", None)
    return jax.shard_map(
        on_device, mesh=mesh, in_specs=in_specs, out_specs=out_specs, check_vma=False
    )
```

profile of v0, /device:TPU:10, one launch (start us, length us, event | category | flops | bytes accessed | tf_op | source)
XLA Modules:
  0.0 271.5 jit_solution(1467407370005647917)
XLA Ops:
  10.2 6.2 %all-to-all-start.1 = ((s32[16,1,3]{2,1,0:T(1,128)}), s32[16,1,3]{2,1,0:T(1,128)S(1)}, u32[]{:S(2)}, u32[]{:S(2)}) async-start(s32[16,1,3]{2,1,0:T(1,128)} %copy.71), calls=%async_computation.1 | async-start | bytes 16384 | tf_op jit(solution)/shard_map/all_to_all | solution.py:101
  17.7 2.0 convolution_convert_fusion.3
  19.7 2.0 convolution_convert_fusion.2
  21.7 2.0 convolution_convert_fusion.1
  24.0 4.2 %convolution_convert_fusion = bf16[16,4,384,128]{3,0,2,1:T(8,128)(2,1)} fusion(bf16[8,4,384,128]{3,2,1,0:T(8,128)(2,1)S(1)} %copy-done.3, s32[8]{0:T(128)S(1)} %get-tuple-element.441), kind=kOutput, calls=%fused_computation.76 | convolution fusion | flops 53477504 | bytes 9437216 | tf_op jit(solution)/shard_map/ej,jhkc->ehkc/dot_general | solution.py:92
  28.9 7.0 %copy.70 = bf16[16,4,384,128]{3,2,1,0:T(8,128)(2,1)} copy(bf16[16,4,384,128]{3,0,2,1:T(8,128)(2,1)} %convolution_convert_fusion) | data formatting | bytes 12582912 | tf_op jit(solution)/shard_map/convert_element_type | solution.py:97
  35.9 6.0 %all-to-all-start = ((bf16[16,4,384,128]{3,2,1,0:T(8,128)(2,1)}), bf16[16,4,384,128]{3,2,1,0:T(8,128)(2,1)}, u32[]{:S(2)}, u32[]{:S(2)}) async-start(bf16[16,4,384,128]{3,2,1,0:T(8,128)(2,1)} %copy.70), calls=%async_computation | async-start | bytes 12582912 | tf_op jit(solution)/shard_map/all_to_all | solution.py:100
  42.0 1.6 broadcast.330.clone.1
  43.6 55.1 %while.34 = (s32[]{:T(128)}, f32[8,4,256]{2,1,0:T(4,128)S(1)}, f32[8,4,256]{2,1,0:T(4,128)S(1)}, f32[8,4,256,64]{2,3,1,0:T(8,128)}, bf16[8,256,4,64]{1,3,2,0:T(8...) while((s32[]{:T(128)}, f32[8,4,256]{2,1,0:T(4,128)S(1)}, ...), condition=%wide.region_4.5_spmd.clone, body=%wide.region_1.4_spmd.clone.sunk | while | flops 175341824 | bytes 18193428 | solution.py:81
  46.4 1.6 fusion.107
  53.4 1.6 fusion.107
  100.1 79.0 %all-to-all-done = bf16[16,4,384,128]{3,2,1,0:T(8,128)(2,1)} async-done(((bf16[16,4,384,128]{3,2,1,0:T(8,128)(2,1)}), bf16[16,4,384,128]{3,2,1,0:T(8,128)(2,1)}, u32[]{:S(2)}, u32[]{:S(2)}) %all-to-all-start) | async-done | bytes 6291488 | tf_op jit(solution)/shard_map/all_to_all | solution.py:100
  179.1 5.6 %gather_fusion = bf16[8,4,384,128]{3,2,1,0:T(8,128)(2,1)} fusion(bf16[16,4,384,128]{3,2,1,0:T(8,128)(2,1)} %all-to-all-done, s32[1024]{0:T(1024)} %pad_clamp_fusion), kind=kCustom, calls=%fused_computation | custom fusion | bytes 6291488 | tf_op jit(solution)/shard_map/jit(_take)/gather | solution.py:103
  184.7 4.0 %broadcast_select_fusion = bf16[8,4,384,128]{3,2,1,0:T(8,128)(2,1)} fusion(bf16[8,4,384,128]{3,2,1,0:T(8,128)(2,1)} %gather_fusion, pred[8]{0:T(512)(128)(4,1)S(1)} %copy-done.7), kind=kLoop, calls=%fused_computation.78 | loop fusion | flops 1572864 | bytes 6291464 | tf_op jit(solution)/shard_map/jit(_take)/select_n | solution.py:103
  188.9 31.4 %while.33 = (s32[]{:T(128)}, f32[8,4,256]{2,1,0:T(4,128)S(1)}, f32[8,4,256]{2,1,0:T(4,128)S(1)}, f32[8,4,256,64]{2,3,1,0:T(8,128)S(1)}, bf16[8,256,4,64]{1,3,2,0...) while((s32[]{:T(128)}, f32[8,4,256]{2,1,0:T(4,128)S(1)}, ...), condition=%wide.region_9.10_spmd, body=%wide.region_6.9_spmd.sunk | while | flops 103907584 | bytes 7903377 | solution.py:105
  220.3 3.3 %divide_convert_fusion = bf16[8,4,256,64]{2,3,1,0:T(8,128)(2,1)} fusion(f32[8,4,256,64]{2,3,1,0:T(8,128)S(1)} %get-tuple-element.256, f32[8,4,256,64]{2,3,1,0:T(8,128)} %get-tuple-element.253, f32[8,4,256]{2,1,0:T(4,128)S(1)} %bitcast.139, f32[8,4,256]{2,1,0:T(4,128)S(1)} %bitcast.141, f32[8,4,256]{2,1,0:T(4,128)S(1)} %bitcast.140), kind=kLoop, calls=%fused_computation.82 | loop fusion | flops 2621440 | bytes 5341184 | tf_op jit(solution)/shard_map/convert_element_type | solution.py:115
  223.6 2.8 %copy.75 = bf16[8,256,256]{2,0,1:T(8,128)(2,1)} copy(bf16[8,256,256]{1,2,0:T(8,128)(2,1)} %bitcast.132) | data formatting | bytes 2097152 | tf_op jit(solution)/shard_map/convert_element_type | solution.py:115
  226.4 4.6 %all-to-all-start.2 = ((bf16[8,256,256]{2,0,1:T(8,128)(2,1)}), bf16[8,256,256]{2,0,1:T(8,128)(2,1)}, u32[]{:S(2)}, u32[]{:S(2)}) async-start(bf16[8,256,256]{2,0,1:T(8,128)(2,1)} %copy.75), calls=%async_computation.2 | async-start | bytes 2097152 | tf_op jit(solution)/shard_map/all_to_all | solution.py:117
  231.0 2.5 convert_element_type.101
  233.6 11.8 %all-to-all-done.2 = bf16[8,256,256]{2,0,1:T(8,128)(2,1)} async-done(((bf16[8,256,256]{2,0,1:T(8,128)(2,1)}), bf16[8,256,256]{2,0,1:T(8,128)(2,1)}, u32[]{:S(2)}, u32[]{:S(2)}) %all-to-all-start.2) | async-done | bytes 1048608 | tf_op jit(solution)/shard_map/all_to_all | solution.py:117
  245.3 2.3 copy.77
  249.1 2.7 multiply_reduce_fusion.1
  253.1 8.6 %fusion.48 = f32[1024,512]{1,0:T(8,128)} fusion(bf16[2048,512]{1,0:T(8,128)(2,1)} %all-gather.5.cloned.1.call-done, bf16[1024,512]{1,0:T(8,128)(2,1)} %bitcast.135, bf16[512,2048]{1,0:T(8,128)(2,1)} %all-gather.3.cloned.1.call-done), kind=kOutput, calls=%fused_computation.75 | convolution fusion | flops 4313841664 | bytes 7340032 | tf_op jit(solution)/shard_map/dot_general | solution.py:134
  261.7 2.9 %add_convert_fusion = bf16[8,128,512]{2,1,0:T(8,128)(2,1)} fusion(f32[8,128,512]{2,1,0:T(8,128)S(1)} %get-tuple-element.455, f32[8,128,512]{2,1,0:T(8,128)} %bitcast.133), kind=kLoop, calls=%fused_computation.79 | loop fusion | flops 1048576 | bytes 5242880 | tf_op jit(solution)/shard_map/convert_element_type | solution.py:139
  (281 shorter events, 92.4 us)
Async XLA Ops:
  6.5 242.6 %copy-start = (bf16[512,512]{1,0:T(8,128)(2,1)S(1)}, bf16[512,512]{1,0:T(8,128)(2,1)}, u32[]{:S(2)}) copy-start(bf16[512,512]{1,0:T(8,128)(2,1)} %param.21) | copy-start | bytes 1572868
  6.5 10.7 %copy-start.1 = (bf16[8,256,512]{2,1,0:T(8,128)(2,1)S(1)}, bf16[8,256,512]{2,1,0:T(8,128)(2,1)}, u32[]{:S(2)}) copy-start(bf16[8,256,512]{2,1,0:T(8,128)(2,1)} %param.15) | copy-start | bytes 6291460
  6.5 11.2 %copy-start.9 = (bf16[3,512,256]{2,1,0:T(8,128)(2,1)S(1)}, bf16[3,512,256]{2,1,0:T(8,128)(2,1)}, u32[]{:S(2)}) copy-start(bf16[3,512,256]{2,1,0:T(8,128)(2,1)} %param.20) | copy-start | bytes 2359300
  6.5 11.2 %copy-start.10 = (f32[512]{0:T(512)S(1)}, f32[512]{0:T(512)}, u32[]{:S(2)}) copy-start(f32[512]{0:T(512)} %param.22) | copy-start | bytes 6148
  6.5 246.5 %all-gather.3.cloned.1.call-start = ((), (), s32[]{:S(2)}) async-start(), calls=%async_computation.3 | async-start | bytes 3145728 | tf_op jit(solution)/shard_map/all_gather | solution.py:130
  10.2 25.8 %all-to-all-start.1 = ((s32[16,1,3]{2,1,0:T(1,128)}), s32[16,1,3]{2,1,0:T(1,128)S(1)}, u32[]{:S(2)}, u32[]{:S(2)}) async-start(s32[16,1,3]{2,1,0:T(1,128)} %copy.71), calls=%async_computation.1 | async-start | bytes 16384 | tf_op jit(solution)/shard_map/all_to_all | solution.py:101
  16.4 236.7 %all-gather.5.cloned.1.call-start = ((), (), s32[]{:S(2)}) async-start(), calls=%async_computation.4 | async-start | bytes 3145728 | tf_op jit(solution)/shard_map/all_gather | solution.py:136
  21.7 2.3 copy-start.3
  24.0 4.2 %copy-start.11 = (f32[4]{0:T(128)S(1)}, f32[4]{0:T(128)}, u32[]{:S(2)}) copy-start(f32[4]{0:T(128)} %param.19) | copy-start | bytes 52
  24.0 4.8 %copy-start.4 = (s32[8,3]{0,1:T(4,128)S(1)}, s32[8,3]{0,1:T(4,128)}, u32[]{:S(2)}) copy-start(s32[8,3]{0,1:T(4,128)} %param.17) | copy-start | bytes 292
  35.9 143.1 %all-to-all-start = ((bf16[16,4,384,128]{3,2,1,0:T(8,128)(2,1)}), bf16[16,4,384,128]{3,2,1,0:T(8,128)(2,1)}, u32[]{:S(2)}, u32[]{:S(2)}) async-start(bf16[16,4,384,128]{3,2,1,0:T(8,128)(2,1)} %copy.70), calls=%async_computation | async-start | bytes 12582912 | tf_op jit(solution)/shard_map/all_to_all | solution.py:100
  43.6 1.0 copy-start.5
  49.5 1.0 copy-start.6
  50.4 1.0 copy-start.5
  57.4 1.0 copy-start.5
  64.3 1.0 copy-start.5
  71.2 1.0 copy-start.5
  78.1 1.0 copy-start.5
  85.0 1.0 copy-start.5
  91.8 1.0 copy-start.5
  100.1 84.6 %copy-start.7 = (pred[8]{0:T(512)(128)(4,1)S(1)}, pred[8]{0:T(512)(128)(4,1)}, u32[]{:S(2)}) copy-start(pred[8]{0:T(512)(128)(4,1)} %get-tuple-element.440) | copy-start | bytes 28
  223.6 7.5 %copy-start.2 = (bf16[8,256,512]{2,1,0:T(8,128)(2,1)S(1)}, bf16[8,256,512]{2,1,0:T(8,128)(2,1)}, u32[]{:S(2)}) copy-start(bf16[8,256,512]{2,1,0:T(8,128)(2,1)} %param.15) | copy-start | bytes 6291460
  226.4 18.9 %all-to-all-start.2 = ((bf16[8,256,256]{2,0,1:T(8,128)(2,1)}), bf16[8,256,256]{2,0,1:T(8,128)(2,1)}, u32[]{:S(2)}, u32[]{:S(2)}) async-start(bf16[8,256,256]{2,0,1:T(8,128)(2,1)} %copy.75), calls=%async_computation.2 | async-start | bytes 2097152 | tf_op jit(solution)/shard_map/all_to_all | solution.py:117
  249.1 2.7 %copy-start.8 = (f32[512]{0:T(512)S(1)}, f32[512]{0:T(512)}, u32[]{:S(2)}) copy-start(f32[512]{0:T(512)} %param.23) | copy-start | bytes 6148
  (7 other events, 6.7 us)
Sparse Core Ops, SparseCore 0:
  8.9 34.2 all-gather.2
  44.7 33.0 all-gather.4
where the time goes:
time: 273 us; the launch traced here: 271 us
  waiting for transfers between devices  92.2 us (34%)
  matrix products  61.1 us (22%)
  local copies, waits for them, and re-layouts  52.4 us (19%)
  other arithmetic  34.2 us (13%)
  starting transfers between devices  17 us (6%)
  between operations  13.6 us (5%)
    all_to_all x1, waiting for transfers between devices, on_device(): lax.all_to_all(send_cache, 'qubit', split_axis=0, concat_axis=0, tiled=True)  79 us
    dot_general x16, matrix products, block_partial(): jnp.einsum('thd,hkd->htk', queries, key_set, preferred_element_type=jnp.f...  23.9 us
    dynamic_slice x32, local copies, waits for them, and re-layouts, on_device(): lax.map(own_partial, (queries, kv_cache, cache_age, fresh_k, fresh_v))  20 us
    dot_general x16, matrix products, block_partial(): jnp.einsum('htk,hkd->htd', weights.astype(jnp.bfloat16), value_set, prefe...  15.6 us
    all_to_all x1, waiting for transfers between devices, on_device(): lax.all_to_all(attended, 'head', split_axis=1, concat_axis=2, tiled=True)  11.8 us
    reduce_sum x16, other arithmetic, block_partial(): return (top, jnp.sum(weights, axis=-1), summed)  11.5 us
    dot_general x1, matrix products, on_device(): jnp.dot(activated, lax.all_gather(w_down, 'head', axis=0, tiled=True), pr...  8.65 us
    transpose x8, local copies, waits for them, and re-layouts, own_partial(): jnp.transpose(value_block, (1, 0, 2))  7.98 us
  transfers between devices with their start and end apart: 5, of which 2 were waited for; matrix products, arithmetic and copies ran while one was open for 50% of the time, Pallas kernels for 0%

commit v1 on v0

v1 whole, which is shorter than its diff:
```python
import functools

import jax
import jax.numpy as jnp
from jax import lax
from jax.experimental import pallas as pl
from jax.experimental.pallas import tpu as pltpu
from jax.sharding import PartitionSpec as P


DH = 64
STAB = 128
F32 = jnp.float32
BF16 = jnp.bfloat16

ANY_SPEC = pl.BlockSpec(memory_space=pl.ANY)
SMEM_SPEC = pl.BlockSpec(memory_space=pltpu.SMEM)


def whole(shape):
    zeros = (0,) * len(shape)
    return pl.BlockSpec(shape, lambda *_: zeros)


def mm(a, b):
    return jnp.dot(a, b, preferred_element_type=F32)


def rms(x, gain):
    return x * lax.rsqrt(jnp.mean(x * x, axis=-1, keepdims=True) + 1e-06) * gain


def cost(flops, nbytes, trans=0):
    return pl.CostEstimate(flops=flops, bytes_accessed=nbytes, transcendentals=trans)


def params():
    return pltpu.CompilerParams(vmem_limit_bytes=48 * 1024 * 1024)


def project_kernel(order_ref, x_ref, gain_ref, w_ref, after_ref, q_ref, k_ref, v_ref):
    normed = rms(x_ref[0].astype(F32), gain_ref[...]).astype(BF16)
    q_ref[...] = mm(normed, w_ref[0]).astype(BF16)
    k_ref[...] = mm(normed, w_ref[1]).astype(BF16)
    v_ref[...] = mm(normed, w_ref[2]).astype(BF16)


def head_attention(queries, parts):
    queries = queries * jnp.asarray(DH**-0.5, BF16)
    lane = lax.broadcasted_iota(jnp.int32, (1, queries.shape[0]), 1)
    blocks = []
    for keys, _, biases, firsts in parts:
        s = lax.dot_general(keys, queries, (((1,), (1,)), ((), ())), preferred_element_type=F32)
        for i, (bias, first) in enumerate(zip(biases, firsts)):
            block = s[i * STAB : (i + 1) * STAB] + bias
            if first:
                block = jnp.where(lane >= first, block, -1e30)
            blocks.append(block)
    top = blocks[0]
    for block in blocks[1:]:
        top = jnp.maximum(top, block)
    top = jnp.max(top, axis=0, keepdims=True)
    weights = [jnp.exp(block - top) for block in blocks]
    total = weights[0]
    for w in weights[1:]:
        total = total + w
    total = jnp.sum(total, axis=0, keepdims=True)
    at, summed = 0, None
    for _, values, biases, _ in parts:
        w = jnp.concatenate([x.astype(BF16) for x in weights[at : at + len(biases)]], axis=0)
        at += len(biases)
        term = lax.dot_general(values, w, (((0,), (0,)), ((), ())), preferred_element_type=F32)
        summed = term if summed is None else summed + term
    return summed / total, top + jnp.log(total)


def cache_part(cache_ref, head, age_ref, row, slope, rounds):
    kv = cache_ref[0, head]
    biases = [-slope * age_ref[row, r].astype(F32) for r in range(rounds)]
    return kv[:, :DH], kv[:, DH:], biases, [0] * rounds


def near_kernel(c, heads, rounds, new_rounds, order_ref, q_ref, k_ref, v_ref, cache_ref, age_ref, slope_ref, after_ref, o_ref):
    row = order_ref[c]
    hd = heads * DH
    for h in range(heads):
        cols = slice(h * DH, (h + 1) * DH)
        slope = slope_ref[h]
        fresh = (
            k_ref[:, cols],
            v_ref[:, cols],
            [slope * float(r) for r in range(new_rounds)],
            [r * STAB for r in range(new_rounds)],
        )
        out, lse = head_attention(q_ref[:, cols], [cache_part(cache_ref, h, age_ref, row, slope, rounds), fresh])
        o_ref[cols, :] = out
        o_ref[hd + h : hd + h + 1, :] = lse


def far_kernel(c, heads, rounds, order_ref, q_ref, cache_ref, age_ref, slope_ref, after_ref, o_ref, lse_scr):
    row = order_ref[c]
    hd = heads * DH
    lse_scr[...] = jnp.zeros_like(lse_scr)
    for h in range(heads):
        cols = slice(h * DH, (h + 1) * DH)
        out, lse = head_attention(q_ref[:, cols], [cache_part(cache_ref, h, age_ref, row, slope_ref[h], rounds)])
        o_ref[cols, :] = out.astype(BF16)
        hi = lse.astype(BF16).astype(F32)
        mid = (lse - hi).astype(BF16).astype(F32)
        lse_scr[h : h + 1, :] = hi
        lse_scr[heads + h : heads + h + 1, :] = mid
        lse_scr[2 * heads + h : 2 * heads + h + 1, :] = lse - hi - mid
    o_ref[hd:, :] = lse_scr[...].astype(BF16)


def join_kernel(heads, pos_ref, near_ref, far_ref, after_ref, *refs):
    outs, scr = refs[:-1], refs[-1]
    hd = heads * DH
    tail = far_ref[hd:, :].astype(F32)
    lse_far = tail[:heads] + tail[heads : 2 * heads] + tail[2 * heads : 3 * heads]
    lse_near = near_ref[hd : hd + heads, :]
    top = jnp.maximum(lse_near, lse_far)
    a, b = jnp.exp(lse_near - top), jnp.exp(lse_far - top)
    a, b = a / (a + b), b / (a + b)
    rows = []
    for h in range(heads):
        cols = slice(h * DH, (h + 1) * DH)
        rows.append(near_ref[cols, :] * a[h : h + 1] + far_ref[cols, :].astype(F32) * b[h : h + 1])
    scr[...] = jnp.transpose(jnp.concatenate(rows, axis=0))
    n, count = len(outs), outs[0].shape[0]
    for r, out in enumerate(outs):
        start = pl.multiple_of(lax.rem(pos_ref[0] + r, n) * count, count)
        out[...] = scr[pl.ds(start, count), :].astype(BF16)


def mlp_kernel(group, n, steps, order_ref, pos_ref, *refs):
    size = len(group)
    pieces = [refs[g * n : (g + 1) * n] for g in range(size)]
    xs = refs[size * n : size * (n + 1)]
    refs = refs[size * (n + 1) :]
    w_os, w_ins, w_downs, gain_ref = refs[:n], refs[n : 2 * n], refs[2 * n : 3 * n], refs[3 * n]
    out_ref, hid, acc, res, sems = refs[-5:]
    rows = pieces[0][0].shape[0]
    step = pl.program_id(0)

    @pl.when(step == 0)
    def _():
        for g in range(size):
            h = xs[g][0].astype(F32)
            for piece, w_o in zip(pieces[g], w_os):
                h += mm(piece[...], w_o[...])
            acc[g * rows : (g + 1) * rows] = h
            hid[g * rows : (g + 1) * rows] = rms(h, gain_ref[...]).astype(BF16)

    x = hid[...]
    total = acc[...]
    for w_in, w_dn in zip(w_ins, w_downs):
        total += mm(jax.nn.gelu(mm(x, w_in[...])).astype(BF16), w_dn[...])
    acc[...] = total

    @pl.when(step == steps - 1)
    def _():
        res[...] = acc[...].astype(BF16).reshape(res.shape)
        copies = [
            pltpu.make_async_copy(res.at[g], out_ref.at[order_ref[c]], sems.at[g]) for g, c in enumerate(group)
        ]
        for copy in copies:
            copy.start()
        for copy in copies:
            copy.wait()


def on_device(n_dev, n, tokens, kv_cache, cache_age, partner, slope, w_qkv, w_o, attn_gain, mlp_gain, w_in, w_down):
    count, new_len, width = tokens.shape
    heads, keys = kv_cache.shape[1], kv_cache.shape[2]
    hd = heads * DH
    rounds, new_rounds = keys // STAB, new_len // STAB
    half = n_dev // 2
    me = lax.axis_index("qubit").astype(jnp.int32)
    pos = lax.axis_index("head").astype(jnp.int32)
    owner = partner // count
    colour = jnp.where(me < half, (owner - me) % half, (me - half - owner) % half)
    slots = jnp.arange(count, dtype=jnp.int32)
    order = jnp.sum(jnp.where(colour[None, :] == slots[:, None], slots[None, :], 0), axis=1).astype(jnp.int32)
    pos1 = pos[None]
    gain1, gain2 = attn_gain[None], mlp_gain[None]
    perms = []
    for c in range(count):
        pairs = [(d, half + (d + c) % half) for d in range(half)]
        perms.append(pairs + [(b, a) for a, b in pairs])
    swaps = [[(a, (a + r) % n) for a in range(n)] for r in range(n)]
    sources = [(pos - r) % n for r in range(n)]
    w_os = [lax.dynamic_slice_in_dim(w_o, src * hd, hd, 0) for src in sources]

    w_ins, w_downs = [w_in], [w_down]
    for r in range(1, n):
        w_ins.append(lax.ppermute(w_in, "head", swaps[r]))
        w_downs.append(lax.ppermute(w_down, "head", swaps[r]))

    after = order
    qs, ks, vs, got_q = [], [], [], []
    one = jax.ShapeDtypeStruct((new_len, hd), BF16)
    for c in range(count):
        q, k, v = pl.pallas_call(
            project_kernel,
            grid_spec=pltpu.PrefetchScalarGridSpec(
                num_scalar_prefetch=1,
                grid=(1,),
                in_specs=[
                    pl.BlockSpec((1, new_len, width), lambda i, o, c=c: (o[c], 0, 0)),
                    whole((1, width)),
                    whole((3, width, hd)),
                    ANY_SPEC,
                ],
                out_specs=[whole((new_len, hd))] * 3,
            ),
            out_shape=[one] * 3,
            compiler_params=params(),
            cost_estimate=cost(6 * new_len * width * hd, 1500000),
        )(order, tokens, gain1, w_qkv, after)
        after = v
        got_q.append(lax.ppermute(q, "qubit", perms[c]))
        qs.append(q)
        ks.append(k)
        vs.append(v)

    near = []
    cache_spec = [pl.BlockSpec((1, heads, keys, 2 * DH), lambda i, o, c=c: (o[c], 0, 0, 0)) for c in range(count)]
    for c in range(count):
        after = pl.pallas_call(
            functools.partial(near_kernel, c, heads, rounds, new_rounds),
            grid_spec=pltpu.PrefetchScalarGridSpec(
                num_scalar_prefetch=1,
                grid=(1,),
                in_specs=[whole((new_len, hd))] * 3 + [cache_spec[c], SMEM_SPEC, SMEM_SPEC, ANY_SPEC],
                out_specs=whole((hd + 8, new_len)),
            ),
            out_shape=jax.ShapeDtypeStruct((hd + 8, new_len), F32),
            compiler_params=params(),
            cost_estimate=cost(4 * heads * new_len * 640 * DH * 4, 1000000),
        )(order, qs[c], ks[c], vs[c], kv_cache, cache_age, slope, after)
        near.append(after)

    back = []
    for c in range(count):
        after = pl.pallas_call(
            functools.partial(far_kernel, c, heads, rounds),
            grid_spec=pltpu.PrefetchScalarGridSpec(
                num_scalar_prefetch=1,
                grid=(1,),
                in_specs=[whole((new_len, hd)), cache_spec[c], SMEM_SPEC, SMEM_SPEC, ANY_SPEC],
                out_specs=whole((hd + 16, new_len)),
                scratch_shapes=[pltpu.VMEM((16, new_len), F32)],
            ),
            out_shape=jax.ShapeDtypeStruct((hd + 16, new_len), BF16),
            compiler_params=params(),
            cost_estimate=cost(4 * heads * new_len * 384 * DH * 4, 1000000),
        )(order, got_q[c], kv_cache, cache_age, slope, after)
        back.append(lax.ppermute(after, "qubit", perms[c]))

    pieces = [None] * count
    rows = new_len // n

    def join(c, after):
        parts = pl.pallas_call(
            functools.partial(join_kernel, heads),
            grid=(1,),
            in_specs=[SMEM_SPEC, whole((hd + 8, new_len)), whole((hd + 16, new_len)), ANY_SPEC],
            out_specs=[whole((rows, hd))] * n,
            out_shape=[jax.ShapeDtypeStruct((rows, hd), BF16)] * n,
            scratch_shapes=[pltpu.VMEM((new_len, hd), F32)],
            compiler_params=params(),
            cost_estimate=cost(1000000, 1000000),
        )(pos1, near[c], back[c], after)
        pieces[c] = [parts[0]] + [lax.ppermute(parts[r], "head", swaps[r]) for r in range(1, n)]
        return parts[0]

    ff = w_in.shape[1]
    steps = 2
    chunk = ff // steps
    out = None

    def mlp(group, out, after):
        size = len(group)
        x_specs = [pl.BlockSpec((1, rows, width), lambda i, o, p, c=c: (o[c], p[0], 0)) for c in group]
        ins = [part for c in group for part in pieces[c]] + [tokens] * size
        ins += w_os + w_ins + w_downs + [gain2, after]
        specs = [whole((rows, hd))] * (n * size) + x_specs + [whole((hd, width))] * n
        specs += [pl.BlockSpec((width, chunk), lambda i, o, p: (0, i))] * n
        specs += [pl.BlockSpec((chunk, width), lambda i, o, p: (i, 0))] * n + [whole((1, width)), ANY_SPEC]
        alias = {}
        if out is not None:
            alias = {len(ins) + 2: 0}
            ins.append(out)
            specs.append(ANY_SPEC)
        return pl.pallas_call(
            functools.partial(mlp_kernel, group, n, steps),
            grid_spec=pltpu.PrefetchScalarGridSpec(
                num_scalar_prefetch=2,
                grid=(steps,),
                in_specs=specs,
                out_specs=ANY_SPEC,
                scratch_shapes=[
                    pltpu.VMEM((size * rows, width), BF16),
                    pltpu.VMEM((size * rows, width), F32),
                    pltpu.VMEM((size, rows, width), BF16),
                    pltpu.SemaphoreType.DMA((size,)),
                ],
            ),
            out_shape=jax.ShapeDtypeStruct((count, rows, width), BF16),
            input_output_aliases=alias,
            compiler_params=params(),
            cost_estimate=cost(size * rows * width * (width + 2 * n * ff) * 2, 5000000),
        )(order, pos1, *ins)

    groups, start = [], 0
    while start < count:
        size = 2 if start < count - 2 else 1
        groups.append(tuple(range(start, min(start + size, count))))
        start += size
    ready = 0
    for group in groups:
        need = min(group[-1] + 2, count)
        while ready < need:
            after = join(ready, after)
            ready += 1
        out = mlp(group, out, after)
        after = out if group is groups[-1] else after
    return out


def solution(mesh):
    in_specs = (
        P("qubit", None, None),
        P("qubit", "head", None, None),
        P("qubit", None),
        P("qubit"),
        P("head"),
        P(None, None, "head"),
        P(),
        P(),
        P(),
        P(None, "head"),
        P("head", None),
    )
    return jax.shard_map(
        functools.partial(on_device, mesh.shape["qubit"], mesh.shape["head"]),
        mesh=mesh,
        in_specs=in_specs,
        out_specs=P("qubit", "head", None),
        check_vma=False,
    )
```

time: 273 us -> 166 us (0.61)
  Pallas kernels: 0 us -> 84.6 us
  matrix products: 61.1 us -> 0 us
  waiting for transfers between devices: 92.2 us -> 31.2 us
  local copies, waits for them, and re-layouts: 52.4 us -> 9.03 us
  other arithmetic: 34.2 us -> 0.79 us
  starting transfers between devices: 17 us -> 39.4 us
  between operations: 13.6 us -> 0.67 us
    all_to_all x3 -> x0, waiting for transfers between devices: 90.8 us -> none  [the longest x1 79 us: on_device(): lax.all_to_all(send_cache, 'qubit', split_axis=0, concat_axis=0, tiled=True)]
    pallas_call x0 -> x37, Pallas kernels: none -> 84.6 us  [the longest x5 26.2 us: mlp(): pl.pallas_call(functools.partial(mlp_kernel, group, n, steps), grid_spec=...]
    dot_general x38 -> x0, matrix products: 61.1 us -> none  [the longest x16 23.9 us: block_partial(): jnp.einsum('thd,hkd->htk', queries, key_set, preferred_element_type=jnp.f...]
    ppermute x0 -> x26, starting transfers between devices: none -> 39.4 us  [the longest x8 14.5 us: on_device(): back.append(lax.ppermute(after, 'qubit', perms[c]))]
    ppermute x0 -> x26, waiting for transfers between devices: none -> 31.2 us  [the longest x8 18.1 us: on_device(): back.append(lax.ppermute(after, 'qubit', perms[c]))]
    dynamic_slice x32 -> x1, local copies, waits for them, and re-layouts: 20 us -> 1.06 us  [on_device(): w_os = [lax.dynamic_slice_in_dim(w_o, src * hd, hd, 0) for src in sources]]
    all_to_all x3 -> x0, starting transfers between devices: 16.9 us -> none  [the longest x1 6.24 us: on_device(): lax.all_to_all(send_age, 'qubit', split_axis=0, concat_axis=0, tiled=True)]
    reduce_sum x18 -> x1, other arithmetic: 12.8 us -> 0.12 us  [on_device(): jnp.sum(jnp.where(colour[None, :] == slots[:, None], slots[None, :], 0),...]
  transfers between devices with their start and end apart: 5 -> 26, of which waited for: 2 -> 6; matrix products, arithmetic and copies ran while one was open for 50% -> 1% of each run, Pallas kernels for 0% -> 47%
where the time goes in v1:
time: 166 us
  Pallas kernels  84.6 us (51%)
  starting transfers between devices  39.4 us (24%)
  waiting for transfers between devices  31.2 us (19%)
  local copies, waits for them, and re-layouts  9.03 us (5%)
    pallas_call x5, Pallas kernels, mlp(): pl.pallas_call(functools.partial(mlp_kernel, group, n, steps), grid_spec=...  26.2 us
    pallas_call x8, Pallas kernels, on_device(): pl.pallas_call(functools.partial(near_kernel, c, heads, rounds, new_round...  23.8 us
    pallas_call x8, Pallas kernels, on_device(): pl.pallas_call(functools.partial(far_kernel, c, heads, rounds), grid_spec...  21.6 us
    ppermute x8, waiting for transfers between devices, on_device(): back.append(lax.ppermute(after, 'qubit', perms[c]))  18.1 us
    ppermute x8, starting transfers between devices, on_device(): back.append(lax.ppermute(after, 'qubit', perms[c]))  14.5 us
    ppermute x8, starting transfers between devices, on_device(): got_q.append(lax.ppermute(q, 'qubit', perms[c]))  13.7 us
    ppermute x8, waiting for transfers between devices, on_device(): got_q.append(lax.ppermute(q, 'qubit', perms[c]))  13 us
    pallas_call x8, Pallas kernels, on_device(): pl.pallas_call(project_kernel, grid_spec=pltpu.PrefetchScalarGridSpec(num...  9.45 us
  transfers between devices with their start and end apart: 26, of which 6 were waited for; matrix products, arithmetic and copies ran while one was open for 1% of the time, Pallas kernels for 47%

profile of v1, /device:TPU:10, one launch (start us, length us, event | category | flops | bytes accessed | tf_op | source)
XLA Modules:
  0.0 165.6 jit_solution(11765056214531948132)
XLA Ops:
  22.0 3.2 %shard_map.117.after_ref.near_ref = f32[264,256]{1,0:T(8,128)S(1)} custom-call(s32[8]{0:T(128)S(1)} %select_reduce_fusion.order_ref.after_ref, bf16[256,256]{1,0:T(8,128)(2,1)} %get-tuple-element.67.q_ref, bf16[256,256]{1,0:T(8,128)(2,1)S(1)} %copy-done.10, bf16[256,256]{1,0:T(8,128)(2,1)S(1)} %get-tuple-element.45.after_ref.v_ref, ...), custom_call_target="tpu_custom_call" | custom-call | flops 671088640 | bytes 1000000 | tf_op jit(solution)/shard_map/pallas_call | solution.py:230
  25.1 3.2 %shard_map.118.after_ref.near_ref = f32[264,256]{1,0:T(8,128)S(1)} custom-call(s32[8]{0:T(128)S(1)} %select_reduce_fusion.order_ref.after_ref, bf16[256,256]{1,0:T(8,128)(2,1)} %get-tuple-element.65.q_ref, bf16[256,256]{1,0:T(8,128)(2,1)S(1)} %copy-done.12, bf16[256,256]{1,0:T(8,128)(2,1)S(1)} %get-tuple-element.46.after_ref.v_ref, ...), custom_call_target="tpu_custom_call" | custom-call | flops 671088640 | bytes 1000000 | tf_op jit(solution)/shard_map/pallas_call | solution.py:230
  28.3 3.2 %shard_map.119.after_ref.near_ref = f32[264,256]{1,0:T(8,128)S(1)} custom-call(s32[8]{0:T(128)S(1)} %select_reduce_fusion.order_ref.after_ref, bf16[256,256]{1,0:T(8,128)(2,1)} %get-tuple-element.63.q_ref, bf16[256,256]{1,0:T(8,128)(2,1)S(1)} %copy-done.14, bf16[256,256]{1,0:T(8,128)(2,1)S(1)} %get-tuple-element.47.after_ref.v_ref, ...), custom_call_target="tpu_custom_call" | custom-call | flops 671088640 | bytes 1000000 | tf_op jit(solution)/shard_map/pallas_call | solution.py:230
  31.5 2.8 %shard_map.120.after_ref.near_ref = f32[264,256]{1,0:T(8,128)S(1)} custom-call(s32[8]{0:T(128)S(1)} %select_reduce_fusion.order_ref.after_ref, bf16[256,256]{1,0:T(8,128)(2,1)S(1)} %get-tuple-element.61.q_ref, bf16[256,256]{1,0:T(8,128)(2,1)S(1)} %get-tuple-element.62.k_ref, bf16[256,256]{1,0:T(8,128)(2,1)S(1)} %get-tuple-element.48.after_ref.v_ref, ...), custom_call_target="tpu_custom_call" | custom-call | flops 671088640 | bytes 1000000 | tf_op jit(solution)/shard_map/pallas_call | solution.py:230
  34.3 2.8 %shard_map.121.after_ref.near_ref = f32[264,256]{1,0:T(8,128)S(1)} custom-call(s32[8]{0:T(128)S(1)} %select_reduce_fusion.order_ref.after_ref, bf16[256,256]{1,0:T(8,128)(2,1)S(1)} %get-tuple-element.59.q_ref, bf16[256,256]{1,0:T(8,128)(2,1)S(1)} %get-tuple-element.60.k_ref, bf16[256,256]{1,0:T(8,128)(2,1)S(1)} %get-tuple-element.49.after_ref.v_ref, ...), custom_call_target="tpu_custom_call" | custom-call | flops 671088640 | bytes 1000000 | tf_op jit(solution)/shard_map/pallas_call | solution.py:230
  37.2 2.8 %shard_map.122.after_ref.near_ref = f32[264,256]{1,0:T(8,128)S(1)} custom-call(s32[8]{0:T(128)S(1)} %select_reduce_fusion.order_ref.after_ref, bf16[256,256]{1,0:T(8,128)(2,1)S(1)} %get-tuple-element.57.q_ref, bf16[256,256]{1,0:T(8,128)(2,1)S(1)} %get-tuple-element.58.k_ref, bf16[256,256]{1,0:T(8,128)(2,1)S(1)} %get-tuple-element.50.after_ref.v_ref, ...), custom_call_target="tpu_custom_call" | custom-call | flops 671088640 | bytes 1000000 | tf_op jit(solution)/shard_map/pallas_call | solution.py:230
  40.0 3.0 %shard_map.123.after_ref.near_ref = f32[264,256]{1,0:T(8,128)S(1)} custom-call(s32[8]{0:T(128)S(1)} %select_reduce_fusion.order_ref.after_ref, bf16[256,256]{1,0:T(8,128)(2,1)S(1)} %get-tuple-element.55.q_ref, bf16[256,256]{1,0:T(8,128)(2,1)S(1)} %get-tuple-element.56.k_ref, bf16[256,256]{1,0:T(8,128)(2,1)S(1)} %get-tuple-element.51.after_ref.v_ref, ...), custom_call_target="tpu_custom_call" | custom-call | flops 671088640 | bytes 1000000 | tf_op jit(solution)/shard_map/pallas_call | solution.py:230
  43.1 2.8 %shard_map.124.after_ref.near_ref = f32[264,256]{1,0:T(8,128)S(1)} custom-call(s32[8]{0:T(128)S(1)} %select_reduce_fusion.order_ref.after_ref, bf16[256,256]{1,0:T(8,128)(2,1)S(1)} %get-tuple-element.52.q_ref, bf16[256,256]{1,0:T(8,128)(2,1)S(1)} %get-tuple-element.53.k_ref, bf16[256,256]{1,0:T(8,128)(2,1)S(1)} %get-tuple-element.54.after_ref.v_ref, ...), custom_call_target="tpu_custom_call" | custom-call | flops 671088640 | bytes 1000000 | tf_op jit(solution)/shard_map/pallas_call | solution.py:230
  46.7 3.0 %shard_map.125.after_ref = bf16[272,256]{1,0:T(8,128)(2,1)S(1)} custom-call(s32[8]{0:T(128)S(1)} %select_reduce_fusion.order_ref.after_ref, bf16[256,256]{1,0:T(8,128)(2,1)} %collective-permute-done.7.q_ref, bf16[8,4,384,128]{3,2,1,0:T(8,128)(2,1)S(1)} %copy-done, s32[8,3]{1,0:T(8,128)S(1)} %copy.39.age_ref, f32[4]{0:T(128)S(1)} %copy-done.17, ...), custom_call_target="tpu_custom_call" | custom-call | flops 402653184 | bytes 1000000 | tf_op jit(solution)/shard_map/pallas_call | solution.py:246
  51.6 2.7 %shard_map.126.after_ref = bf16[272,256]{1,0:T(8,128)(2,1)S(1)} custom-call(s32[8]{0:T(128)S(1)} %select_reduce_fusion.order_ref.after_ref, bf16[256,256]{1,0:T(8,128)(2,1)S(1)} %collective-permute-done.6.q_ref, bf16[8,4,384,128]{3,2,1,0:T(8,128)(2,1)S(1)} %copy-done, s32[8,3]{1,0:T(8,128)S(1)} %copy.39.age_ref, f32[4]{0:T(128)S(1)} %copy-done.17, ...), custom_call_target="tpu_custom_call" | custom-call | flops 402653184 | bytes 1000000 | tf_op jit(solution)/shard_map/pallas_call | solution.py:246
  54.3 3.6 %collective-permute-start.1 = (bf16[256,256]{1,0:T(8,128)(2,1)S(1)}, bf16[256,256]{1,0:T(8,128)(2,1)S(1)}, u32[]{:S(2)}, u32[]{:S(2)}) collective-permute-start(bf16[256,256]{1,0:T(8,128)(2,1)S(1)} %get-tuple-element.55.q_ref), channel_id=1, source_target_pairs={{0,28},{2,30},{4,16},{6,18},{8,20},{10,22},{12,24},{14,26},{28,0},... | collective-permute-start | bytes 393224 | tf_op jit(solution)/shard_map/ppermute | solution.py:222
  60.5 2.7 %shard_map.128.after_ref = bf16[272,256]{1,0:T(8,128)(2,1)S(1)} custom-call(s32[8]{0:T(128)S(1)} %select_reduce_fusion.order_ref.after_ref, bf16[256,256]{1,0:T(8,128)(2,1)S(1)} %collective-permute-done.4.q_ref, bf16[8,4,384,128]{3,2,1,0:T(8,128)(2,1)S(1)} %copy-done, s32[8,3]{1,0:T(8,128)S(1)} %copy.39.age_ref, f32[4]{0:T(128)S(1)} %copy-done.17, ...), custom_call_target="tpu_custom_call" | custom-call | flops 402653184 | bytes 1000000 | tf_op jit(solution)/shard_map/pallas_call | solution.py:246
  63.2 2.7 %shard_map.129.after_ref = bf16[272,256]{1,0:T(8,128)(2,1)S(1)} custom-call(s32[8]{0:T(128)S(1)} %select_reduce_fusion.order_ref.after_ref, bf16[256,256]{1,0:T(8,128)(2,1)S(1)} %collective-permute-done.3.q_ref, bf16[8,4,384,128]{3,2,1,0:T(8,128)(2,1)S(1)} %copy-done, s32[8,3]{1,0:T(8,128)S(1)} %copy.39.age_ref, f32[4]{0:T(128)S(1)} %copy-done.17, ...), custom_call_target="tpu_custom_call" | custom-call | flops 402653184 | bytes 1000000 | tf_op jit(solution)/shard_map/pallas_call | solution.py:246
  68.6 2.7 %shard_map.131.after_ref = bf16[272,256]{1,0:T(8,128)(2,1)S(1)} custom-call(s32[8]{0:T(128)S(1)} %select_reduce_fusion.order_ref.after_ref, bf16[256,256]{1,0:T(8,128)(2,1)S(1)} %collective-permute-done.1.q_ref, bf16[8,4,384,128]{3,2,1,0:T(8,128)(2,1)S(1)} %copy-done, s32[8,3]{1,0:T(8,128)S(1)} %copy.39.age_ref, f32[4]{0:T(128)S(1)} %copy-done.17, ...), custom_call_target="tpu_custom_call" | custom-call | flops 402653184 | bytes 1000000 | tf_op jit(solution)/shard_map/pallas_call | solution.py:246
  75.5 13.0 %collective-permute-done.q_ref = bf16[256,256]{1,0:T(8,128)(2,1)S(1)} collective-permute-done((bf16[256,256]{1,0:T(8,128)(2,1)S(1)}, bf16[256,256]{1,0:T(8,128)(2,1)S(1)}, u32[]{:S(2)}, u32[]{:S(2)}) %collective-permute-start) | collective-permute-done | bytes 131104 | tf_op jit(solution)/shard_map/ppermute | solution.py:222
  89.9 3.7 %collective-permute-start.14 = (bf16[272,256]{1,0:T(8,128)(2,1)S(1)}, bf16[272,256]{1,0:T(8,128)(2,1)S(1)}, u32[]{:S(2)}, u32[]{:S(2)}) collective-permute-start(bf16[272,256]{1,0:T(8,128)(2,1)S(1)} %shard_map.126.after_ref), channel_id=1, source_target_pairs={{0,18},{2,20},{4,22},{6,24},{8,26},{10,28},{12,30},{14,16},{18,0},... | collective-permute-start | bytes 417800 | tf_op jit(solution)/shard_map/ppermute | solution.py:259
  94.8 9.2 %collective-permute-done.11.far_ref = bf16[272,256]{1,0:T(8,128)(2,1)S(1)} collective-permute-done((bf16[272,256]{1,0:T(8,128)(2,1)S(1)}, bf16[272,256]{1,0:T(8,128)(2,1)S(1)}, u32[]{:S(2)}, u32[]{:S(2)}) %collective-permute-start.11) | collective-permute-done | bytes 139296 | tf_op jit(solution)/shard_map/ppermute | solution.py:259
  104.0 4.1 %collective-permute-start.12 = (bf16[272,256]{1,0:T(8,128)(2,1)S(1)}, bf16[272,256]{1,0:T(8,128)(2,1)}, u32[]{:S(2)}, u32[]{:S(2)}) collective-permute-start(bf16[272,256]{1,0:T(8,128)(2,1)S(1)} %shard_map.128.after_ref), channel_id=1, source_target_pairs={{0,22},{2,24},{4,26},{6,28},{8,30},{10,16},{12,18},{14,20},{22,0},... | collective-permute-start | bytes 417800 | tf_op jit(solution)/shard_map/ppermute | solution.py:259
  122.4 4.9 %collective-permute-done.13.far_ref = bf16[272,256]{1,0:T(8,128)(2,1)} collective-permute-done((bf16[272,256]{1,0:T(8,128)(2,1)S(1)}, bf16[272,256]{1,0:T(8,128)(2,1)}, u32[]{:S(2)}, u32[]{:S(2)}) %collective-permute-start.13) | collective-permute-done | bytes 139296 | tf_op jit(solution)/shard_map/ppermute | solution.py:259
  137.6 5.5 %shard_map.141.refs_14_ = bf16[8,128,512]{2,1,0:T(8,128)(2,1)} custom-call(s32[8]{0:T(128)S(1)} %select_reduce_fusion.order_ref.after_ref, s32[1]{0:T(128)} %bitcast.pos_ref, bf16[128,256]{1,0:T(8,128)(2,1)S(1)} %get-tuple-element.69.after_ref.refs_0_, bf16[128,256]{1,0:T(8,128)(2,1)S(1)} %collective-permute-done.24.refs_1_, ...), custom_call_target="tpu_custom_call" | custom-call | flops 1207959552 | bytes 5000000 | tf_op jit(solution)/shard_map/pallas_call | solution.py:296
  144.7 5.5 %shard_map.142.refs_14_ = bf16[8,128,512]{2,1,0:T(8,128)(2,1)} custom-call(s32[8]{0:T(128)S(1)} %select_reduce_fusion.order_ref.after_ref, s32[1]{0:T(128)} %bitcast.pos_ref, bf16[128,256]{1,0:T(8,128)(2,1)S(1)} %get-tuple-element.71.after_ref.refs_13_.refs_0_, ...), custom_call_target="tpu_custom_call", output_to_operand_aliasing={{}: (16, {})} | custom-call | flops 1207959552 | bytes 5000000 | tf_op jit(solution)/shard_map/pallas_call | solution.py:296
  150.3 5.5 %shard_map.143.refs_11_ = bf16[8,128,512]{2,1,0:T(8,128)(2,1)} custom-call(s32[8]{0:T(128)S(1)} %select_reduce_fusion.order_ref.after_ref, s32[1]{0:T(128)} %bitcast.pos_ref, bf16[128,256]{1,0:T(8,128)(2,1)S(1)} %get-tuple-element.73.after_ref.refs_13_.refs_0_, ...), custom_call_target="tpu_custom_call", output_to_operand_aliasing={{}: (16, {})} | custom-call | flops 1207959552 | bytes 5000000 | tf_op jit(solution)/shard_map/pallas_call | solution.py:296
  155.8 4.8 %shard_map.144.refs_11_ = bf16[8,128,512]{2,1,0:T(8,128)(2,1)} custom-call(s32[8]{0:T(128)S(1)} %select_reduce_fusion.order_ref.after_ref, s32[1]{0:T(128)} %bitcast.pos_ref, bf16[128,256]{1,0:T(8,128)(2,1)S(1)} %get-tuple-element.75.after_ref.refs_13_.refs_0_, ...), custom_call_target="tpu_custom_call", output_to_operand_aliasing={{}: (13, {})} | custom-call | flops 603979776 | bytes 5000000 | tf_op jit(solution)/shard_map/pallas_call | solution.py:296
  160.7 4.8 %shard_map.145 = bf16[8,128,512]{2,1,0:T(8,128)(2,1)} custom-call(s32[8]{0:T(128)S(1)} %select_reduce_fusion.order_ref.after_ref, s32[1]{0:T(128)} %bitcast.pos_ref, bf16[128,256]{1,0:T(8,128)(2,1)S(1)} %get-tuple-element.76.refs_10_.refs_0_, bf16[128,256]{1,0:T(8,128)(2,1)S(1)} %collective-permute-done.16.refs_1_, ...), custom_call_target="tpu_custom_call", output_to_operand_aliasing={{}: (13, {})} | custom-call | flops 603979776 | bytes 5000000 | tf_op jit(solution)/shard_map/pallas_call | solution.py:296
  (109 shorter events, 62.8 us)
Async XLA Ops:
  6.4 36.6 %collective-permute-start.7 = (bf16[256,256]{1,0:T(8,128)(2,1)}, bf16[256,256]{1,0:T(8,128)(2,1)}, u32[]{:S(2)}, u32[]{:S(2)}) collective-permute-start(bf16[256,256]{1,0:T(8,128)(2,1)} %get-tuple-element.67.q_ref), channel_id=1, source_target_pairs={{0,16},{2,18},{4,20},{6,22},{8,24},{10,26},{12,28},{14,30},{16,0},... | collective-permute-start | bytes 393224 | tf_op jit(solution)/shard_map/ppermute | solution.py:222
  10.5 35.4 %collective-permute-start.6 = (bf16[256,256]{1,0:T(8,128)(2,1)}, bf16[256,256]{1,0:T(8,128)(2,1)S(1)}, u32[]{:S(2)}, u32[]{:S(2)}) collective-permute-start(bf16[256,256]{1,0:T(8,128)(2,1)} %get-tuple-element.65.q_ref), channel_id=1, source_target_pairs={{0,18},{2,20},{4,22},{6,24},{8,26},{10,28},{12,30},{14,16},{18,0},... | collective-permute-start | bytes 393224 | tf_op jit(solution)/shard_map/ppermute | solution.py:222
  12.7 37.0 %collective-permute-start.5 = (bf16[256,256]{1,0:T(8,128)(2,1)}, bf16[256,256]{1,0:T(8,128)(2,1)S(1)}, u32[]{:S(2)}, u32[]{:S(2)}) collective-permute-start(bf16[256,256]{1,0:T(8,128)(2,1)} %get-tuple-element.63.q_ref), channel_id=1, source_target_pairs={{0,20},{2,22},{4,24},{6,26},{8,28},{10,30},{12,16},{14,18},{20,0},... | collective-permute-start | bytes 393224 | tf_op jit(solution)/shard_map/ppermute | solution.py:222
  14.8 120.7 %collective-permute-start.17 = (bf16[512,1024]{1,0:T(8,128)(2,1)}, bf16[512,1024]{1,0:T(8,128)(2,1)}, u32[]{:S(2)}, u32[]{:S(2)}) collective-permute-start(bf16[512,1024]{1,0:T(8,128)(2,1)} %refs_5_.9), channel_id=1, source_target_pairs={{0,1},{1,0},{2,3},{3,2},{4,5},{5,4},{6,7},{7,6},{8,9},{9,8},{10,11... | collective-permute-start | bytes 3145736 | tf_op jit(solution)/shard_map/ppermute | solution.py:197
  16.3 120.7 %collective-permute-start.18 = (bf16[1024,512]{1,0:T(8,128)(2,1)}, bf16[1024,512]{1,0:T(8,128)(2,1)}, u32[]{:S(2)}, u32[]{:S(2)}) collective-permute-start(bf16[1024,512]{1,0:T(8,128)(2,1)} %refs_7_.3), channel_id=1, source_target_pairs={{0,1},{1,0},{2,3},{3,2},{4,5},{5,4},{6,7},{7,6},{8,9},{9,8},{10,11... | collective-permute-start | bytes 3145736 | tf_op jit(solution)/shard_map/ppermute | solution.py:198
  43.0 11.2 %collective-permute-start.4 = (bf16[256,256]{1,0:T(8,128)(2,1)S(1)}, bf16[256,256]{1,0:T(8,128)(2,1)S(1)}, u32[]{:S(2)}, u32[]{:S(2)}) collective-permute-start(bf16[256,256]{1,0:T(8,128)(2,1)S(1)} %get-tuple-element.61.q_ref), channel_id=1, source_target_pairs={{0,22},{2,24},{4,26},{6,28},{8,30},{10,16},{12,18},{14,20},{22,0},... | collective-permute-start | bytes 393224 | tf_op jit(solution)/shard_map/ppermute | solution.py:222
  46.0 17.3 %collective-permute-start.3 = (bf16[256,256]{1,0:T(8,128)(2,1)S(1)}, bf16[256,256]{1,0:T(8,128)(2,1)S(1)}, u32[]{:S(2)}, u32[]{:S(2)}) collective-permute-start(bf16[256,256]{1,0:T(8,128)(2,1)S(1)} %get-tuple-element.59.q_ref), channel_id=1, source_target_pairs={{0,24},{2,26},{4,28},{6,30},{8,16},{10,18},{12,20},{14,22},{24,0},... | collective-permute-start | bytes 393224 | tf_op jit(solution)/shard_map/ppermute | solution.py:222
  49.7 16.2 %collective-permute-start.2 = (bf16[256,256]{1,0:T(8,128)(2,1)S(1)}, bf16[256,256]{1,0:T(8,128)(2,1)S(1)}, u32[]{:S(2)}, u32[]{:S(2)}) collective-permute-start(bf16[256,256]{1,0:T(8,128)(2,1)S(1)} %get-tuple-element.57.q_ref), channel_id=1, source_target_pairs={{0,26},{2,28},{4,30},{6,16},{8,18},{10,20},{12,22},{14,24},{26,0},... | collective-permute-start | bytes 393224 | tf_op jit(solution)/shard_map/ppermute | solution.py:222
  54.3 14.3 %collective-permute-start.1 = (bf16[256,256]{1,0:T(8,128)(2,1)S(1)}, bf16[256,256]{1,0:T(8,128)(2,1)S(1)}, u32[]{:S(2)}, u32[]{:S(2)}) collective-permute-start(bf16[256,256]{1,0:T(8,128)(2,1)S(1)} %get-tuple-element.55.q_ref), channel_id=1, source_target_pairs={{0,28},{2,30},{4,16},{6,18},{8,20},{10,22},{12,24},{14,26},{28,0},... | collective-permute-start | bytes 393224 | tf_op jit(solution)/shard_map/ppermute | solution.py:222
  71.3 18.6 %collective-permute-start.9 = (bf16[272,256]{1,0:T(8,128)(2,1)S(1)}, bf16[272,256]{1,0:T(8,128)(2,1)S(1)}, u32[]{:S(2)}, u32[]{:S(2)}) collective-permute-start(bf16[272,256]{1,0:T(8,128)(2,1)S(1)} %shard_map.131.after_ref), channel_id=1, source_target_pairs={{0,28},{2,30},{4,16},{6,18},{8,20},{10,22},{12,24},{14,26},{28,0},... | collective-permute-start | bytes 417800 | tf_op jit(solution)/shard_map/ppermute | solution.py:259
  72.9 15.6 %collective-permute-start = (bf16[256,256]{1,0:T(8,128)(2,1)S(1)}, bf16[256,256]{1,0:T(8,128)(2,1)S(1)}, u32[]{:S(2)}, u32[]{:S(2)}) collective-permute-start(bf16[256,256]{1,0:T(8,128)(2,1)S(1)} %get-tuple-element.52.q_ref), channel_id=1, source_target_pairs={{0,30},{2,16},{4,18},{6,20},{8,22},{10,24},{12,26},{14,28},{30,0},... | collective-permute-start | bytes 393224 | tf_op jit(solution)/shard_map/ppermute | solution.py:222
  75.5 18.1 %collective-permute-start.10 = (bf16[272,256]{1,0:T(8,128)(2,1)S(1)}, bf16[272,256]{1,0:T(8,128)(2,1)S(1)}, u32[]{:S(2)}, u32[]{:S(2)}) collective-permute-start(bf16[272,256]{1,0:T(8,128)(2,1)S(1)} %shard_map.130.after_ref), channel_id=1, source_target_pairs={{0,26},{2,28},{4,30},{6,16},{8,18},{10,20},{12,22},{14,24},{26,0},... | collective-permute-start | bytes 417800 | tf_op jit(solution)/shard_map/ppermute | solution.py:259
  88.5 15.5 %collective-permute-start.11 = (bf16[272,256]{1,0:T(8,128)(2,1)S(1)}, bf16[272,256]{1,0:T(8,128)(2,1)S(1)}, u32[]{:S(2)}, u32[]{:S(2)}) collective-permute-start(bf16[272,256]{1,0:T(8,128)(2,1)S(1)} %shard_map.129.after_ref), channel_id=1, source_target_pairs={{0,24},{2,26},{4,28},{6,30},{8,16},{10,18},{12,20},{14,22},{24,0},... | collective-permute-start | bytes 417800 | tf_op jit(solution)/shard_map/ppermute | solution.py:259
  89.9 19.4 %collective-permute-start.14 = (bf16[272,256]{1,0:T(8,128)(2,1)S(1)}, bf16[272,256]{1,0:T(8,128)(2,1)S(1)}, u32[]{:S(2)}, u32[]{:S(2)}) collective-permute-start(bf16[272,256]{1,0:T(8,128)(2,1)S(1)} %shard_map.126.after_ref), channel_id=1, source_target_pairs={{0,18},{2,20},{4,22},{6,24},{8,26},{10,28},{12,30},{14,16},{18,0},... | collective-permute-start | bytes 417800 | tf_op jit(solution)/shard_map/ppermute | solution.py:259
  93.6 21.7 %collective-permute-start.15 = (bf16[272,256]{1,0:T(8,128)(2,1)S(1)}, bf16[272,256]{1,0:T(8,128)(2,1)S(1)}, u32[]{:S(2)}, u32[]{:S(2)}) collective-permute-start(bf16[272,256]{1,0:T(8,128)(2,1)S(1)} %shard_map.125.after_ref), channel_id=1, source_target_pairs={{0,16},{2,18},{4,20},{6,22},{8,24},{10,26},{12,28},{14,30},{16,0},... | collective-permute-start | bytes 417800 | tf_op jit(solution)/shard_map/ppermute | solution.py:259
  104.0 16.9 %collective-permute-start.12 = (bf16[272,256]{1,0:T(8,128)(2,1)S(1)}, bf16[272,256]{1,0:T(8,128)(2,1)}, u32[]{:S(2)}, u32[]{:S(2)}) collective-permute-start(bf16[272,256]{1,0:T(8,128)(2,1)S(1)} %shard_map.128.after_ref), channel_id=1, source_target_pairs={{0,22},{2,24},{4,26},{6,28},{8,30},{10,16},{12,18},{14,20},{22,0},... | collective-permute-start | bytes 417800 | tf_op jit(solution)/shard_map/ppermute | solution.py:259
  109.9 17.3 %collective-permute-start.13 = (bf16[272,256]{1,0:T(8,128)(2,1)S(1)}, bf16[272,256]{1,0:T(8,128)(2,1)}, u32[]{:S(2)}, u32[]{:S(2)}) collective-permute-start(bf16[272,256]{1,0:T(8,128)(2,1)S(1)} %shard_map.127.after_ref), channel_id=1, source_target_pairs={{0,20},{2,22},{4,24},{6,26},{8,28},{10,30},{12,16},{14,18},{20,0},... | collective-permute-start | bytes 417800 | tf_op jit(solution)/shard_map/ppermute | solution.py:259
  116.0 16.7 %collective-permute-start.8 = (bf16[272,256]{1,0:T(8,128)(2,1)S(1)}, bf16[272,256]{1,0:T(8,128)(2,1)S(1)}, u32[]{:S(2)}, u32[]{:S(2)}) collective-permute-start(bf16[272,256]{1,0:T(8,128)(2,1)S(1)} %shard_map.132.after_ref), channel_id=1, source_target_pairs={{0,30},{2,16},{4,18},{6,20},{8,22},{10,24},{12,26},{14,28},{30,0},... | collective-permute-start | bytes 417800 | tf_op jit(solution)/shard_map/ppermute | solution.py:259
  120.9 12.7 %collective-permute-start.25 = (bf16[128,256]{1,0:T(8,128)(2,1)S(1)}, bf16[128,256]{1,0:T(8,128)(2,1)S(1)}, u32[]{:S(2)}, u32[]{:S(2)}) collective-permute-start(bf16[128,256]{1,0:T(8,128)(2,1)S(1)} %get-tuple-element.84), channel_id=1, source_target_pairs={{0,1},{1,0},{2,3},{3,2},{4,5},{5,4},{6,7},{7,6},{8,9},{9,8},{10,11... | collective-permute-start | bytes 196616 | tf_op jit(solution)/shard_map/ppermute | solution.py:275
  127.3 7.8 %collective-permute-start.24 = (bf16[128,256]{1,0:T(8,128)(2,1)S(1)}, bf16[128,256]{1,0:T(8,128)(2,1)S(1)}, u32[]{:S(2)}, u32[]{:S(2)}) collective-permute-start(bf16[128,256]{1,0:T(8,128)(2,1)S(1)} %get-tuple-element.83), channel_id=1, source_target_pairs={{0,1},{1,0},{2,3},{3,2},{4,5},{5,4},{6,7},{7,6},{8,9},{9,8},{10,11... | collective-permute-start | bytes 196616 | tf_op jit(solution)/shard_map/ppermute | solution.py:275
  132.9 27.7 %collective-permute-start.16 = (bf16[128,256]{1,0:T(8,128)(2,1)S(1)}, bf16[128,256]{1,0:T(8,128)(2,1)S(1)}, u32[]{:S(2)}, u32[]{:S(2)}) collective-permute-start(bf16[128,256]{1,0:T(8,128)(2,1)S(1)} %get-tuple-element.77), channel_id=1, source_target_pairs={{0,1},{1,0},{2,3},{3,2},{4,5},{5,4},{6,7},{7,6},{8,9},{9,8},{10,11... | collective-permute-start | bytes 196616 | tf_op jit(solution)/shard_map/ppermute | solution.py:275
  133.5 22.3 %collective-permute-start.19 = (bf16[128,256]{1,0:T(8,128)(2,1)S(1)}, bf16[128,256]{1,0:T(8,128)(2,1)S(1)}, u32[]{:S(2)}, u32[]{:S(2)}) collective-permute-start(bf16[128,256]{1,0:T(8,128)(2,1)S(1)} %get-tuple-element.78), channel_id=1, source_target_pairs={{0,1},{1,0},{2,3},{3,2},{4,5},{5,4},{6,7},{7,6},{8,9},{9,8},{10,11... | collective-permute-start | bytes 196616 | tf_op jit(solution)/shard_map/ppermute | solution.py:275
  135.0 15.2 %collective-permute-start.21 = (bf16[128,256]{1,0:T(8,128)(2,1)S(1)}, bf16[128,256]{1,0:T(8,128)(2,1)S(1)}, u32[]{:S(2)}, u32[]{:S(2)}) collective-permute-start(bf16[128,256]{1,0:T(8,128)(2,1)S(1)} %get-tuple-element.80), channel_id=1, source_target_pairs={{0,1},{1,0},{2,3},{3,2},{4,5},{5,4},{6,7},{7,6},{8,9},{9,8},{10,11... | collective-permute-start | bytes 196616 | tf_op jit(solution)/shard_map/ppermute | solution.py:275
  137.1 7.6 %collective-permute-start.22 = (bf16[128,256]{1,0:T(8,128)(2,1)S(1)}, bf16[128,256]{1,0:T(8,128)(2,1)S(1)}, u32[]{:S(2)}, u32[]{:S(2)}) collective-permute-start(bf16[128,256]{1,0:T(8,128)(2,1)S(1)} %get-tuple-element.81), channel_id=1, source_target_pairs={{0,1},{1,0},{2,3},{3,2},{4,5},{5,4},{6,7},{7,6},{8,9},{9,8},{10,11... | collective-permute-start | bytes 196616 | tf_op jit(solution)/shard_map/ppermute | solution.py:275
  (22 other events, 109.5 us)

commit v2 on v1

v2 whole, which is shorter than its diff:
```python
import functools

import jax
import jax.numpy as jnp
from jax import lax
from jax.experimental import pallas as pl
from jax.experimental.pallas import tpu as pltpu
from jax.sharding import PartitionSpec as P


DH = 64
STAB = 128
F32 = jnp.float32
BF16 = jnp.bfloat16

PROJ = 4
GROUP = 2
VMEM_BYTES = 67043328
ANY_SPEC = pl.BlockSpec(memory_space=pl.ANY)
SMEM_SPEC = pl.BlockSpec(memory_space=pltpu.SMEM)


def whole(shape):
    zeros = (0,) * len(shape)
    return pl.BlockSpec(shape, lambda *_: zeros)


def mm(a, b):
    return jnp.dot(a, b, preferred_element_type=F32)


def rms(x, gain):
    return x * lax.rsqrt(jnp.mean(x * x, axis=-1, keepdims=True) + 1e-06) * gain


def cost(flops, nbytes, trans=0):
    return pl.CostEstimate(flops=flops, bytes_accessed=nbytes, transcendentals=trans)


def params():
    return pltpu.CompilerParams(vmem_limit_bytes=VMEM_BYTES)


def project_kernel(size, order_ref, x_ref, gain_ref, w_ref, after_ref, qkv_ref, *q_refs):
    step = pl.program_id(0)
    normed = rms(x_ref[0].astype(F32), gain_ref[...]).astype(BF16)
    q = mm(normed, w_ref[0]).astype(BF16)
    qkv_ref[0, 0] = q
    qkv_ref[0, 1] = mm(normed, w_ref[1]).astype(BF16)
    qkv_ref[0, 2] = mm(normed, w_ref[2]).astype(BF16)
    for g in range(size):

        @pl.when(step == g)
        def _(g=g):
            q_refs[g][...] = q


def head_attention(queries, parts):
    queries = queries * jnp.asarray(DH**-0.5, BF16)
    lane = lax.broadcasted_iota(jnp.int32, (1, queries.shape[0]), 1)
    blocks = []
    for keys, _, biases, firsts in parts:
        s = lax.dot_general(keys, queries, (((1,), (1,)), ((), ())), preferred_element_type=F32)
        for i, (bias, first) in enumerate(zip(biases, firsts)):
            block = s[i * STAB : (i + 1) * STAB] + bias
            if first:
                block = jnp.where(lane >= first, block, -1e30)
            blocks.append(block)
    top = blocks[0]
    for block in blocks[1:]:
        top = jnp.maximum(top, block)
    top = jnp.max(top, axis=0, keepdims=True)
    weights = [jnp.exp(block - top) for block in blocks]
    total = weights[0]
    for w in weights[1:]:
        total = total + w
    total = jnp.sum(total, axis=0, keepdims=True)
    at, summed = 0, None
    for _, values, biases, _ in parts:
        w = jnp.concatenate([x.astype(BF16) for x in weights[at : at + len(biases)]], axis=0)
        at += len(biases)
        term = lax.dot_general(values, w, (((0,), (0,)), ((), ())), preferred_element_type=F32)
        summed = term if summed is None else summed + term
    return summed / total, top + jnp.log(total)


def cache_part(cache_ref, head, age_ref, row, slope, rounds):
    kv = cache_ref[0, head]
    biases = [-slope * age_ref[row, r].astype(F32) for r in range(rounds)]
    return kv[:, :DH], kv[:, DH:], biases, [0] * rounds


def near_kernel(first, heads, rounds, new_rounds, order_ref, qkv_ref, cache_ref, age_ref, slope_ref, after_ref, o_ref):
    row = order_ref[pl.program_id(0) + first]
    hd = heads * DH
    for h in range(heads):
        cols = slice(h * DH, (h + 1) * DH)
        slope = slope_ref[h]
        fresh = (
            qkv_ref[0, 1, :, cols],
            qkv_ref[0, 2, :, cols],
            [slope * float(r) for r in range(new_rounds)],
            [r * STAB for r in range(new_rounds)],
        )
        out, lse = head_attention(qkv_ref[0, 0, :, cols], [cache_part(cache_ref, h, age_ref, row, slope, rounds), fresh])
        o_ref[0, cols, :] = out
        o_ref[0, hd + h : hd + h + 1, :] = lse


def far_kernel(first, size, heads, rounds, order_ref, *refs):
    q_refs = refs[:size]
    cache_ref, age_ref, slope_ref, _ = refs[size : size + 4]
    o_refs, (out_scr, lse_scr) = refs[size + 4 : 2 * size + 4], refs[-2:]
    step = pl.program_id(0)
    row = order_ref[first + step]
    hd = heads * DH
    lse_scr[...] = jnp.zeros_like(lse_scr)
    for h in range(heads):
        cols = slice(h * DH, (h + 1) * DH)
        q = q_refs[0][:, cols]
        for g in range(1, size):
            q = jnp.where(step == g, q_refs[g][:, cols], q)
        out, lse = head_attention(q, [cache_part(cache_ref, h, age_ref, row, slope_ref[h], rounds)])
        out_scr[cols, :] = out.astype(BF16)
        hi = lse.astype(BF16).astype(F32)
        mid = (lse - hi).astype(BF16).astype(F32)
        lse_scr[h : h + 1, :] = hi
        lse_scr[heads + h : heads + h + 1, :] = mid
        lse_scr[2 * heads + h : 2 * heads + h + 1, :] = lse - hi - mid
    out_scr[hd:, :] = lse_scr[...].astype(BF16)
    for g in range(size):

        @pl.when(step == g)
        def _(g=g):
            o_refs[g][...] = out_scr[...]


def join_kernel(size, heads, pos_ref, near_ref, *refs):
    far_refs, outs, scr = refs[:size], refs[size + 1 : -1], refs[-1]
    hd = heads * DH
    for g, far_ref in enumerate(far_refs):
        tail = far_ref[hd:, :].astype(F32)
        lse_far = tail[:heads] + tail[heads : 2 * heads] + tail[2 * heads : 3 * heads]
        lse_near = near_ref[g, hd : hd + heads, :]
        top = jnp.maximum(lse_near, lse_far)
        a, b = jnp.exp(lse_near - top), jnp.exp(lse_far - top)
        a, b = a / (a + b), b / (a + b)
        rows = []
        for h in range(heads):
            cols = slice(h * DH, (h + 1) * DH)
            rows.append(near_ref[g, cols, :] * a[h : h + 1] + far_ref[cols, :].astype(F32) * b[h : h + 1])
        scr[...] = jnp.transpose(jnp.concatenate(rows, axis=0))
        n, count = len(outs), outs[0].shape[1]
        for r, out in enumerate(outs):
            start = pl.multiple_of(lax.rem(pos_ref[0] + r, n) * count, count)
            out[g] = scr[pl.ds(start, count), :].astype(BF16)


def mlp_kernel(group, n, steps, order_ref, pos_ref, *refs):
    size = len(group)
    pieces, xs, refs = refs[:n], refs[n : n + size], refs[n + size :]
    w_os, w_ins, w_downs, gain_ref = refs[:n], refs[n : 2 * n], refs[2 * n : 3 * n], refs[3 * n]
    out_ref, hid, acc, res, sems = refs[-5:]
    rows = pieces[0].shape[1]
    step = pl.program_id(0)

    @pl.when(step == 0)
    def _():
        for g in range(size):
            h = xs[g][0].astype(F32)
            for piece, w_o in zip(pieces, w_os):
                h += mm(piece[g], w_o[...])
            acc[g * rows : (g + 1) * rows] = h
            hid[g * rows : (g + 1) * rows] = rms(h, gain_ref[...]).astype(BF16)

    x = hid[...]
    total = acc[...]
    for w_in, w_dn in zip(w_ins, w_downs):
        total += mm(jax.nn.gelu(mm(x, w_in[...])).astype(BF16), w_dn[...])
    acc[...] = total

    @pl.when(step == steps - 1)
    def _():
        res[...] = acc[...].astype(BF16).reshape(res.shape)
        copies = [
            pltpu.make_async_copy(res.at[g], out_ref.at[order_ref[c]], sems.at[g]) for g, c in enumerate(group)
        ]
        for copy in copies:
            copy.start()
        for copy in copies:
            copy.wait()


def on_device(n_dev, n, tokens, kv_cache, cache_age, partner, slope, w_qkv, w_o, attn_gain, mlp_gain, w_in, w_down):
    count, new_len, width = tokens.shape
    heads, keys = kv_cache.shape[1], kv_cache.shape[2]
    hd = heads * DH
    rounds, new_rounds = keys // STAB, new_len // STAB
    half = n_dev // 2
    me = lax.axis_index("qubit").astype(jnp.int32)
    pos = lax.axis_index("head").astype(jnp.int32)
    owner = partner // count
    colour = jnp.where(me < half, (owner - me) % half, (me - half - owner) % half)
    slots = jnp.arange(count, dtype=jnp.int32)
    order = jnp.sum(jnp.where(colour[None, :] == slots[:, None], slots[None, :], 0), axis=1).astype(jnp.int32)
    pos1 = pos[None]
    gain1, gain2 = attn_gain[None], mlp_gain[None]
    perms = []
    for c in range(count):
        pairs = [(d, half + (d + c) % half) for d in range(half)]
        perms.append(pairs + [(b, a) for a, b in pairs])
    swaps = [[(a, (a + r) % n) for a in range(n)] for r in range(n)]
    sources = [(pos - r) % n for r in range(n)]
    w_os = [lax.dynamic_slice_in_dim(w_o, src * hd, hd, 0) for src in sources]

    w_ins, w_downs = [w_in], [w_down]
    for r in range(1, n):
        w_ins.append(lax.ppermute(w_in, "head", swaps[r]))
        w_downs.append(lax.ppermute(w_down, "head", swaps[r]))

    after = order
    got_q = []
    block = jax.ShapeDtypeStruct((new_len, hd), BF16)
    qkvs, nears = [], []
    for first in range(0, count, PROJ):
        qkv, *qs = pl.pallas_call(
            functools.partial(project_kernel, PROJ),
            grid_spec=pltpu.PrefetchScalarGridSpec(
                num_scalar_prefetch=1,
                grid=(PROJ,),
                in_specs=[
                    pl.BlockSpec((1, new_len, width), lambda i, o, f=first: (o[f + i], 0, 0)),
                    whole((1, width)),
                    whole((3, width, hd)),
                    ANY_SPEC,
                ],
                out_specs=[pl.BlockSpec((1, 3, new_len, hd), lambda i, o: (i, 0, 0, 0))]
                + [whole((new_len, hd))] * PROJ,
            ),
            out_shape=[jax.ShapeDtypeStruct((PROJ, 3, new_len, hd), BF16)] + [block] * PROJ,
            compiler_params=params(),
            cost_estimate=cost(6 * PROJ * new_len * width * hd, 1500000 * PROJ),
        )(order, tokens, gain1, w_qkv, after)
        after = qkv
        qkvs.append(qkv)
        for g in range(PROJ):
            got_q.append(lax.ppermute(qs[g], "qubit", perms[first + g]))

    def cache_spec(first):
        return pl.BlockSpec((1, heads, keys, 2 * DH), lambda i, o: (o[first + i], 0, 0, 0))

    for first in range(0, count, PROJ):
        after = pl.pallas_call(
            functools.partial(near_kernel, first, heads, rounds, new_rounds),
            grid_spec=pltpu.PrefetchScalarGridSpec(
                num_scalar_prefetch=1,
                grid=(PROJ,),
                in_specs=[
                    pl.BlockSpec((1, 3, new_len, hd), lambda i, o: (i, 0, 0, 0)),
                    cache_spec(first),
                    SMEM_SPEC,
                    SMEM_SPEC,
                    ANY_SPEC,
                ],
                out_specs=pl.BlockSpec((1, hd + 8, new_len), lambda i, o: (i, 0, 0)),
            ),
            out_shape=jax.ShapeDtypeStruct((PROJ, hd + 8, new_len), F32),
            compiler_params=params(),
            cost_estimate=cost(16 * PROJ * heads * new_len * 640 * DH, 1000000 * PROJ),
        )(order, qkvs[first // PROJ], kv_cache, cache_age, slope, after)
        nears.append(after)

    back = []
    for first in range(0, count, GROUP):
        fars = pl.pallas_call(
            functools.partial(far_kernel, first, GROUP, heads, rounds),
            grid_spec=pltpu.PrefetchScalarGridSpec(
                num_scalar_prefetch=1,
                grid=(GROUP,),
                in_specs=[whole((new_len, hd))] * GROUP + [cache_spec(first), SMEM_SPEC, SMEM_SPEC, ANY_SPEC],
                out_specs=[whole((hd + 16, new_len))] * GROUP,
                scratch_shapes=[pltpu.VMEM((hd + 16, new_len), BF16), pltpu.VMEM((16, new_len), F32)],
            ),
            out_shape=[jax.ShapeDtypeStruct((hd + 16, new_len), BF16)] * GROUP,
            compiler_params=params(),
            cost_estimate=cost(16 * GROUP * heads * new_len * 384 * DH, 1000000 * GROUP),
        )(order, *got_q[first : first + GROUP], kv_cache, cache_age, slope, after)
        after = fars[0]
        for g in range(GROUP):
            back.append(lax.ppermute(fars[g], "qubit", perms[first + g]))

    rows = new_len // n

    def join(first, after):
        slot = (first % PROJ) // GROUP
        parts = pl.pallas_call(
            functools.partial(join_kernel, GROUP, heads),
            grid=(1,),
            in_specs=[SMEM_SPEC, pl.BlockSpec((GROUP, hd + 8, new_len), lambda i: (slot, 0, 0))]
            + [whole((hd + 16, new_len))] * GROUP
            + [ANY_SPEC],
            out_specs=[whole((GROUP, rows, hd))] * n,
            out_shape=[jax.ShapeDtypeStruct((GROUP, rows, hd), BF16)] * n,
            scratch_shapes=[pltpu.VMEM((new_len, hd), F32)],
            compiler_params=params(),
            cost_estimate=cost(1000000 * GROUP, 1000000 * GROUP),
        )(pos1, nears[first // PROJ], *back[first : first + GROUP], after)
        pieces = [parts[0]] + [lax.ppermute(parts[r], "head", swaps[r]) for r in range(1, n)]
        return pieces, parts[0]

    ff = w_in.shape[1]
    steps = 2
    chunk = ff // steps
    out = None

    def mlp(group, pieces, out, after):
        size = len(group)
        x_specs = [pl.BlockSpec((1, rows, width), lambda i, o, p, c=c: (o[c], p[0], 0)) for c in group]
        ins = pieces + [tokens] * size
        ins += w_os + w_ins + w_downs + [gain2, after]
        specs = [whole((size, rows, hd))] * n + x_specs + [whole((hd, width))] * n
        specs += [pl.BlockSpec((width, chunk), lambda i, o, p: (0, i))] * n
        specs += [pl.BlockSpec((chunk, width), lambda i, o, p: (i, 0))] * n + [whole((1, width)), ANY_SPEC]
        alias = {}
        if out is not None:
            alias = {len(ins) + 2: 0}
            ins.append(out)
            specs.append(ANY_SPEC)
        return pl.pallas_call(
            functools.partial(mlp_kernel, group, n, steps),
            grid_spec=pltpu.PrefetchScalarGridSpec(
                num_scalar_prefetch=2,
                grid=(steps,),
                in_specs=specs,
                out_specs=ANY_SPEC,
                scratch_shapes=[
                    pltpu.VMEM((size * rows, width), BF16),
                    pltpu.VMEM((size * rows, width), F32),
                    pltpu.VMEM((size, rows, width), BF16),
                    pltpu.SemaphoreType.DMA((size,)),
                ],
            ),
            out_shape=jax.ShapeDtypeStruct((count, rows, width), BF16),
            input_output_aliases=alias,
            compiler_params=params(),
            cost_estimate=cost(size * rows * width * (width + 2 * n * ff) * 2, 5000000),
        )(order, pos1, *ins)

    pieces, after = join(0, after)
    for first in range(0, count, GROUP):
        here = pieces
        if first + GROUP < count:
            pieces, after = join(first + GROUP, after)
        out = mlp(tuple(range(first, first + GROUP)), here, out, after)
        after = out
    return out


def solution(mesh):
    in_specs = (
        P("qubit", None, None),
        P("qubit", "head", None, None),
        P("qubit", None),
        P("qubit"),
        P("head"),
        P(None, None, "head"),
        P(),
        P(),
        P(),
        P(None, "head"),
        P("head", None),
    )
    return jax.shard_map(
        functools.partial(on_device, mesh.shape["qubit"], mesh.shape["head"]),
        mesh=mesh,
        in_specs=in_specs,
        out_specs=P("qubit", "head", None),
        check_vma=False,
    )
```

time: 166 us -> 136 us (0.82)
  waiting for transfers between devices: 31.2 us -> 7.26 us
  starting transfers between devices: 39.4 us -> 35.4 us
  local copies, waits for them, and re-layouts: 9.03 us -> 5.5 us
    ppermute x16, waiting for transfers between devices: 31.1 us -> 7.23 us  [the longest x8 4.34 us: on_device(): got_q.append(lax.ppermute(qs[g], 'qubit', perms[first + g]))]
    unnamed x41 -> x2, local copies, waits for them, and re-layouts: 7.96 us -> 3.61 us
    ppermute x8 -> x4, starting transfers between devices: 9.23 us -> 5.05 us  [join(): lax.ppermute(parts[r], 'head', swaps[r])]
    pallas_call x32 -> x12, Pallas kernels: 58.3 us -> 60.8 us  [the longest x4 22.4 us: on_device(): pl.pallas_call(functools.partial(far_kernel, first, GROUP, heads, rounds)...]
    pallas_call x5 -> x4, Pallas kernels: 26.2 us -> 24 us  [mlp(): pl.pallas_call(functools.partial(mlp_kernel, group, n, steps), grid_spec=...]
  transfers between devices with their start and end apart: 26 -> 22, of which waited for: 6 -> 5; matrix products, arithmetic and copies ran while one was open for 1% -> 4% of each run, Pallas kernels for 47% -> 50%
where the time goes in v2:
time: 136 us; the launch traced here: 135 us
  Pallas kernels  84.8 us (62%)
  starting transfers between devices  35.4 us (26%)
  waiting for transfers between devices  7.26 us (5%)
  local copies, waits for them, and re-layouts  5.5 us (4%)
  other arithmetic  1.37 us (1%)
    pallas_call x4, Pallas kernels, mlp(): pl.pallas_call(functools.partial(mlp_kernel, group, n, steps), grid_spec=...  24 us
    pallas_call x4, Pallas kernels, on_device(): pl.pallas_call(functools.partial(far_kernel, first, GROUP, heads, rounds)...  22.4 us
    pallas_call x2, Pallas kernels, on_device(): pl.pallas_call(functools.partial(near_kernel, first, heads, rounds, new_r...  18.8 us
    ppermute x8, starting transfers between devices, on_device(): back.append(lax.ppermute(fars[g], 'qubit', perms[first + g]))  14.9 us
    ppermute x8, starting transfers between devices, on_device(): got_q.append(lax.ppermute(qs[g], 'qubit', perms[first + g]))  13.4 us
    pallas_call x2, Pallas kernels, on_device(): pl.pallas_call(functools.partial(project_kernel, PROJ), grid_spec=pltpu.P...  11 us
    pallas_call x4, Pallas kernels, join(): pl.pallas_call(functools.partial(join_kernel, GROUP, heads), grid=(1,), i...  8.53 us
    ppermute x4, starting transfers between devices, join(): lax.ppermute(parts[r], 'head', swaps[r])  5.05 us
  transfers between devices with their start and end apart: 22, of which 5 were waited for; matrix products, arithmetic and copies ran while one was open for 4% of the time, Pallas kernels for 50%

profile of v2, /device:TPU:10, one launch (start us, length us, event | category | flops | bytes accessed | tf_op | source)
XLA Modules:
  0.0 134.6 jit_solution(16824454216852177215)
XLA Ops:
  1.4 5.5 %shard_map.109 = (bf16[4,3,256,256]{3,2,1,0:T(8,128)(2,1)}, bf16[256,256]{1,0:T(8,128)(2,1)}, bf16[256,256]{1,0:T(8,128)(2,1)}, bf16[256,256]{1,0:T(8,128)(2,1)}, bf16[256,256]{1,0:T(8,128)(2,1)}) custom-call(s32[8]{0:T(128)} %select_reduce_fusion.order_ref.after_ref, bf16[8,256,512]{2,1,0:T(8,128)(2,1)} %refs_3_.11, f32[1,512]{1,0:T(1,128)} %bitcast.7, ...), custom_call_target="tpu_custom_call" | custom-call | flops 805306368 | bytes 6000000 | tf_op jit(solution)/shard_map/pallas_call | solution.py:226
  6.9 5.6 %shard_map.110 = (bf16[4,3,256,256]{3,2,1,0:T(8,128)(2,1)}, bf16[256,256]{1,0:T(8,128)(2,1)}, bf16[256,256]{1,0:T(8,128)(2,1)}, bf16[256,256]{1,0:T(8,128)(2,1)}, bf16[256,256]{1,0:T(8,128)(2,1)}) custom-call(s32[8]{0:T(128)} %select_reduce_fusion.order_ref.after_ref, bf16[8,256,512]{2,1,0:T(8,128)(2,1)} %refs_3_.11, f32[1,512]{1,0:T(1,128)} %bitcast.8, ...), custom_call_target="tpu_custom_call" | custom-call | flops 805306368 | bytes 6000000 | tf_op jit(solution)/shard_map/pallas_call | solution.py:226
  12.4 2.6 %collective-permute-start = (bf16[256,256]{1,0:T(8,128)(2,1)}, bf16[256,256]{1,0:T(8,128)(2,1)}, u32[]{:S(2)}, u32[]{:S(2)}) collective-permute-start(bf16[256,256]{1,0:T(8,128)(2,1)} %get-tuple-element.33), channel_id=1, source_target_pairs={{0,28},{2,30},{4,16},{6,18},{8,20},{10,22},{12,24},{14,26},{28,0},... | collective-permute-start | bytes 393224 | tf_op jit(solution)/shard_map/ppermute | solution.py:247
  15.0 2.8 %collective-permute-start.6 = (bf16[256,256]{1,0:T(8,128)(2,1)}, bf16[256,256]{1,0:T(8,128)(2,1)}, u32[]{:S(2)}, u32[]{:S(2)}) collective-permute-start(bf16[256,256]{1,0:T(8,128)(2,1)} %get-tuple-element.39), channel_id=1, source_target_pairs={{0,16},{2,18},{4,20},{6,22},{8,24},{10,26},{12,28},{14,30},{16,0},... | collective-permute-start | bytes 393224 | tf_op jit(solution)/shard_map/ppermute | solution.py:247
  21.2 9.4 %shard_map.111.after_ref.near_ref = f32[4,264,256]{2,1,0:T(8,128)} custom-call(s32[8]{0:T(128)} %select_reduce_fusion.order_ref.after_ref, bf16[4,3,256,256]{3,2,1,0:T(8,128)(2,1)} %get-tuple-element.31.after_ref.qkv_ref, bf16[8,4,384,128]{3,2,1,0:T(8,128)(2,1)} %refs_2_.11, s32[8,3]{1,0:T(8,128)} %copy.22.age_ref.refs_3_, f32[4]{0:T(128)} %refs_4_.7, ...), custom_call_target="tpu_custom_call" | custom-call | flops 2684354560 | bytes 4000000 | tf_op jit(solution)/shard_map/pallas_call | solution.py:253
  32.1 3.2 %collective-permute-start.7 = (bf16[256,256]{1,0:T(8,128)(2,1)}, bf16[256,256]{1,0:T(8,128)(2,1)}, u32[]{:S(2)}, u32[]{:S(2)}) collective-permute-start(bf16[256,256]{1,0:T(8,128)(2,1)} %get-tuple-element.40), channel_id=1, source_target_pairs={{0,18},{2,20},{4,22},{6,24},{8,26},{10,28},{12,30},{14,16},{18,0},... | collective-permute-start | bytes 393224 | tf_op jit(solution)/shard_map/ppermute | solution.py:247
  35.2 9.4 %shard_map.112.refs_5_.near_ref = f32[4,264,256]{2,1,0:T(8,128)} custom-call(s32[8]{0:T(128)} %select_reduce_fusion.order_ref.after_ref, bf16[4,3,256,256]{3,2,1,0:T(8,128)(2,1)} %get-tuple-element.32.after_ref.qkv_ref, bf16[8,4,384,128]{3,2,1,0:T(8,128)(2,1)} %refs_2_.11, s32[8,3]{1,0:T(8,128)} %copy.22.age_ref.refs_3_, f32[4]{0:T(128)} %refs_4_.7, ...), custom_call_target="tpu_custom_call" | custom-call | flops 2684354560 | bytes 4000000 | tf_op jit(solution)/shard_map/pallas_call | solution.py:253
  44.6 4.2 %collective-permute-done.7.refs_1_ = bf16[256,256]{1,0:T(8,128)(2,1)} collective-permute-done((bf16[256,256]{1,0:T(8,128)(2,1)}, bf16[256,256]{1,0:T(8,128)(2,1)}, u32[]{:S(2)}, u32[]{:S(2)}) %collective-permute-start.7) | collective-permute-done | bytes 131104 | tf_op jit(solution)/shard_map/ppermute | solution.py:247
  48.8 5.6 %shard_map.113 = (bf16[272,256]{1,0:T(8,128)(2,1)}, bf16[272,256]{1,0:T(8,128)(2,1)}) custom-call(s32[8]{0:T(128)} %select_reduce_fusion.order_ref.after_ref, bf16[256,256]{1,0:T(8,128)(2,1)} %collective-permute-done.6.refs_0_, bf16[256,256]{1,0:T(8,128)(2,1)} %collective-permute-done.7.refs_1_, bf16[8,4,384,128]{3,2,1,0:T(8,128)(2,1)} %refs_2_.11, ...), custom_call_target="tpu_custom_call" | custom-call | flops 805306368 | bytes 2000000 | tf_op jit(solution)/shard_map/pallas_call | solution.py:275
  54.4 3.5 %collective-permute-start.1 = (bf16[256,256]{1,0:T(8,128)(2,1)}, bf16[256,256]{1,0:T(8,128)(2,1)}, u32[]{:S(2)}, u32[]{:S(2)}) collective-permute-start(bf16[256,256]{1,0:T(8,128)(2,1)} %get-tuple-element.34), channel_id=1, source_target_pairs={{0,30},{2,16},{4,18},{6,20},{8,22},{10,24},{12,26},{14,28},{30,0},... | collective-permute-start | bytes 393224 | tf_op jit(solution)/shard_map/ppermute | solution.py:247
  59.8 5.6 %shard_map.114 = (bf16[272,256]{1,0:T(8,128)(2,1)}, bf16[272,256]{1,0:T(8,128)(2,1)}) custom-call(s32[8]{0:T(128)} %select_reduce_fusion.order_ref.after_ref, bf16[256,256]{1,0:T(8,128)(2,1)} %collective-permute-done.4.refs_0_, bf16[256,256]{1,0:T(8,128)(2,1)} %collective-permute-done.5.refs_1_, bf16[8,4,384,128]{3,2,1,0:T(8,128)(2,1)} %refs_2_.11, ...), custom_call_target="tpu_custom_call" | custom-call | flops 805306368 | bytes 2000000 | tf_op jit(solution)/shard_map/pallas_call | solution.py:275
  65.4 2.3 %collective-permute-start.13 = (bf16[272,256]{1,0:T(8,128)(2,1)}, bf16[272,256]{1,0:T(8,128)(2,1)}, u32[]{:S(2)}, u32[]{:S(2)}) collective-permute-start(bf16[272,256]{1,0:T(8,128)(2,1)} %get-tuple-element.47), channel_id=1, source_target_pairs={{0,18},{2,20},{4,22},{6,24},{8,26},{10,28},{12,30},{14,16},{18,0},... | collective-permute-start | bytes 417800 | tf_op jit(solution)/shard_map/ppermute | solution.py:290
  67.7 5.6 %shard_map.115 = (bf16[272,256]{1,0:T(8,128)(2,1)}, bf16[272,256]{1,0:T(8,128)(2,1)}) custom-call(s32[8]{0:T(128)} %select_reduce_fusion.order_ref.after_ref, bf16[256,256]{1,0:T(8,128)(2,1)} %collective-permute-done.2.refs_0_, bf16[256,256]{1,0:T(8,128)(2,1)} %collective-permute-done.3.refs_1_, bf16[8,4,384,128]{3,2,1,0:T(8,128)(2,1)} %refs_2_.11, ...), custom_call_target="tpu_custom_call" | custom-call | flops 805306368 | bytes 2000000 | tf_op jit(solution)/shard_map/pallas_call | solution.py:275
  75.6 5.6 %shard_map.116 = (bf16[272,256]{1,0:T(8,128)(2,1)}, bf16[272,256]{1,0:T(8,128)(2,1)}) custom-call(s32[8]{0:T(128)} %select_reduce_fusion.order_ref.after_ref, bf16[256,256]{1,0:T(8,128)(2,1)} %collective-permute-done.refs_0_, bf16[256,256]{1,0:T(8,128)(2,1)} %collective-permute-done.1.refs_1_, bf16[8,4,384,128]{3,2,1,0:T(8,128)(2,1)} %refs_2_.11, ...), custom_call_target="tpu_custom_call" | custom-call | flops 805306368 | bytes 2000000 | tf_op jit(solution)/shard_map/pallas_call | solution.py:275
  82.2 2.1 %shard_map.117 = (bf16[2,128,256]{2,1,0:T(8,128)(2,1)}, bf16[2,128,256]{2,1,0:T(8,128)(2,1)}) custom-call(s32[1]{0:T(128)} %bitcast.pos_ref, f32[4,264,256]{2,1,0:T(8,128)} %shard_map.111.after_ref.near_ref, bf16[272,256]{1,0:T(8,128)(2,1)} %collective-permute-done.12.refs_0_, bf16[272,256]{1,0:T(8,128)(2,1)} %collective-permute-done.13.refs_1_, ...), custom_call_target="tpu_custom_call" | custom-call | flops 2000000 | bytes 2000000 | tf_op jit(solution)/shard_map/pallas_call | solution.py:296
  88.4 2.1 %shard_map.118 = (bf16[2,128,256]{2,1,0:T(8,128)(2,1)}, bf16[2,128,256]{2,1,0:T(8,128)(2,1)}) custom-call(s32[1]{0:T(128)} %bitcast.pos_ref, f32[4,264,256]{2,1,0:T(8,128)} %shard_map.111.after_ref.near_ref, bf16[272,256]{1,0:T(8,128)(2,1)} %collective-permute-done.10.refs_0_, bf16[272,256]{1,0:T(8,128)(2,1)} %collective-permute-done.11.refs_1_, ...), custom_call_target="tpu_custom_call" | custom-call | flops 2000000 | bytes 2000000 | tf_op jit(solution)/shard_map/pallas_call | solution.py:296
  93.9 7.9 %collective-permute-start.8 = (bf16[272,256]{1,0:T(8,128)(2,1)}, bf16[272,256]{1,0:T(8,128)(2,1)}, u32[]{:S(2)}, u32[]{:S(2)}) collective-permute-start(bf16[272,256]{1,0:T(8,128)(2,1)} %get-tuple-element.44.refs_2_), channel_id=1, source_target_pairs={{0,28},{2,30},{4,16},{6,18},{8,20},{10,22},{12,24},{14,26},{28,0},... | collective-permute-start | bytes 417800 | tf_op jit(solution)/shard_map/ppermute | solution.py:290
  101.8 6.0 %shard_map.119.refs_2_.refs_12_ = bf16[8,128,512]{2,1,0:T(8,128)(2,1)} custom-call(s32[8]{0:T(128)} %select_reduce_fusion.order_ref.after_ref, s32[1]{0:T(128)} %bitcast.pos_ref, bf16[2,128,256]{2,1,0:T(8,128)(2,1)} %get-tuple-element.48.refs_2_.refs_0_, bf16[2,128,256]{2,1,0:T(8,128)(2,1)} %collective-permute-done.19.refs_1_, ...), custom_call_target="tpu_custom_call" | custom-call | flops 1207959552 | bytes 5000000 | tf_op jit(solution)/shard_map/pallas_call | solution.py:329
  107.8 2.1 %shard_map.120 = (bf16[2,128,256]{2,1,0:T(8,128)(2,1)}, bf16[2,128,256]{2,1,0:T(8,128)(2,1)}) custom-call(s32[1]{0:T(128)} %bitcast.pos_ref, f32[4,264,256]{2,1,0:T(8,128)} %shard_map.112.refs_5_.near_ref, bf16[272,256]{1,0:T(8,128)(2,1)} %collective-permute-done.17.refs_0_, bf16[272,256]{1,0:T(8,128)(2,1)} %collective-permute-done.18.refs_1_, ...), custom_call_target="tpu_custom_call" | custom-call | flops 2000000 | bytes 2000000 | tf_op jit(solution)/shard_map/pallas_call | solution.py:296
  110.0 6.1 %shard_map.121.refs_2_.refs_12_ = bf16[8,128,512]{2,1,0:T(8,128)(2,1)} custom-call(s32[8]{0:T(128)} %select_reduce_fusion.order_ref.after_ref, s32[1]{0:T(128)} %bitcast.pos_ref, bf16[2,128,256]{2,1,0:T(8,128)(2,1)} %get-tuple-element.49.refs_11_.refs_0_, bf16[2,128,256]{2,1,0:T(8,128)(2,1)} %collective-permute-done.14.refs_1_, ...), custom_call_target="tpu_custom_call", output_to_operand_aliasing={{}: (14, {})} | custom-call | flops 1207959552 | bytes 5000000 | tf_op jit(solution)/shard_map/pallas_call | solution.py:329
  116.1 2.1 %shard_map.122 = (bf16[2,128,256]{2,1,0:T(8,128)(2,1)}, bf16[2,128,256]{2,1,0:T(8,128)(2,1)}) custom-call(s32[1]{0:T(128)} %bitcast.pos_ref, f32[4,264,256]{2,1,0:T(8,128)} %shard_map.112.refs_5_.near_ref, bf16[272,256]{1,0:T(8,128)(2,1)} %collective-permute-done.8.refs_0_, bf16[272,256]{1,0:T(8,128)(2,1)} %collective-permute-done.9.refs_1_, ...), custom_call_target="tpu_custom_call" | custom-call | flops 2000000 | bytes 2000000 | tf_op jit(solution)/shard_map/pallas_call | solution.py:296
  120.3 5.9 %shard_map.123.refs_11_ = bf16[8,128,512]{2,1,0:T(8,128)(2,1)} custom-call(s32[8]{0:T(128)} %select_reduce_fusion.order_ref.after_ref, s32[1]{0:T(128)} %bitcast.pos_ref, bf16[2,128,256]{2,1,0:T(8,128)(2,1)} %get-tuple-element.53.refs_11_.refs_0_, bf16[2,128,256]{2,1,0:T(8,128)(2,1)} %collective-permute-done.21.refs_1_, ...), custom_call_target="tpu_custom_call", output_to_operand_aliasing={{}: (14, {})} | custom-call | flops 1207959552 | bytes 5000000 | tf_op jit(solution)/shard_map/pallas_call | solution.py:329
  126.2 2.3 %copy.29.refs_12_ = bf16[8,128,512]{2,1,0:T(8,128)(2,1)} copy(bf16[8,128,512]{2,1,0:T(8,128)(2,1)} %shard_map.123.refs_11_) | data formatting | bytes 2097152
  128.5 5.9 %shard_map.124 = bf16[8,128,512]{2,1,0:T(8,128)(2,1)} custom-call(s32[8]{0:T(128)} %select_reduce_fusion.order_ref.after_ref, s32[1]{0:T(128)} %bitcast.pos_ref, bf16[2,128,256]{2,1,0:T(8,128)(2,1)} %get-tuple-element.54.refs_11_.refs_0_, bf16[2,128,256]{2,1,0:T(8,128)(2,1)} %collective-permute-done.20.refs_1_, ...), custom_call_target="tpu_custom_call", output_to_operand_aliasing={{}: (14, {})} | custom-call | flops 1207959552 | bytes 5000000 | tf_op jit(solution)/shard_map/pallas_call | solution.py:329
  (41 shorter events, 20.8 us)
Async XLA Ops:
  12.4 18.1 %collective-permute-start = (bf16[256,256]{1,0:T(8,128)(2,1)}, bf16[256,256]{1,0:T(8,128)(2,1)}, u32[]{:S(2)}, u32[]{:S(2)}) collective-permute-start(bf16[256,256]{1,0:T(8,128)(2,1)} %get-tuple-element.33), channel_id=1, source_target_pairs={{0,28},{2,30},{4,16},{6,18},{8,20},{10,22},{12,24},{14,26},{28,0},... | collective-permute-start | bytes 393224 | tf_op jit(solution)/shard_map/ppermute | solution.py:247
  15.0 17.0 %collective-permute-start.2 = (bf16[256,256]{1,0:T(8,128)(2,1)}, bf16[256,256]{1,0:T(8,128)(2,1)}, u32[]{:S(2)}, u32[]{:S(2)}) collective-permute-start(bf16[256,256]{1,0:T(8,128)(2,1)} %get-tuple-element.35), channel_id=1, source_target_pairs={{0,24},{2,26},{4,28},{6,30},{8,16},{10,18},{12,20},{14,22},{24,0},... | collective-permute-start | bytes 393224 | tf_op jit(solution)/shard_map/ppermute | solution.py:247
  15.0 17.1 %collective-permute-start.6 = (bf16[256,256]{1,0:T(8,128)(2,1)}, bf16[256,256]{1,0:T(8,128)(2,1)}, u32[]{:S(2)}, u32[]{:S(2)}) collective-permute-start(bf16[256,256]{1,0:T(8,128)(2,1)} %get-tuple-element.39), channel_id=1, source_target_pairs={{0,16},{2,18},{4,20},{6,22},{8,24},{10,26},{12,28},{14,30},{16,0},... | collective-permute-start | bytes 393224 | tf_op jit(solution)/shard_map/ppermute | solution.py:247
  17.8 76.1 %collective-permute-start.15 = (bf16[512,1024]{1,0:T(8,128)(2,1)}, bf16[512,1024]{1,0:T(8,128)(2,1)}, u32[]{:S(2)}, u32[]{:S(2)}) collective-permute-start(bf16[512,1024]{1,0:T(8,128)(2,1)} %refs_6_.7), channel_id=1, source_target_pairs={{0,1},{1,0},{2,3},{3,2},{4,5},{5,4},{6,7},{7,6},{8,9},{9,8},{10,11... | collective-permute-start | bytes 3145736 | tf_op jit(solution)/shard_map/ppermute | solution.py:218
  19.3 82.5 %collective-permute-start.16 = (bf16[1024,512]{1,0:T(8,128)(2,1)}, bf16[1024,512]{1,0:T(8,128)(2,1)}, u32[]{:S(2)}, u32[]{:S(2)}) collective-permute-start(bf16[1024,512]{1,0:T(8,128)(2,1)} %refs_8_.7), channel_id=1, source_target_pairs={{0,1},{1,0},{2,3},{3,2},{4,5},{5,4},{6,7},{7,6},{8,9},{9,8},{10,11... | collective-permute-start | bytes 3145736 | tf_op jit(solution)/shard_map/ppermute | solution.py:219
  30.6 23.9 %collective-permute-start.4 = (bf16[256,256]{1,0:T(8,128)(2,1)}, bf16[256,256]{1,0:T(8,128)(2,1)}, u32[]{:S(2)}, u32[]{:S(2)}) collective-permute-start(bf16[256,256]{1,0:T(8,128)(2,1)} %get-tuple-element.37), channel_id=1, source_target_pairs={{0,20},{2,22},{4,24},{6,26},{8,28},{10,30},{12,16},{14,18},{20,0},... | collective-permute-start | bytes 393224 | tf_op jit(solution)/shard_map/ppermute | solution.py:247
  31.9 26.0 %collective-permute-start.5 = (bf16[256,256]{1,0:T(8,128)(2,1)}, bf16[256,256]{1,0:T(8,128)(2,1)}, u32[]{:S(2)}, u32[]{:S(2)}) collective-permute-start(bf16[256,256]{1,0:T(8,128)(2,1)} %get-tuple-element.38), channel_id=1, source_target_pairs={{0,22},{2,24},{4,26},{6,28},{8,30},{10,16},{12,18},{14,20},{22,0},... | collective-permute-start | bytes 393224 | tf_op jit(solution)/shard_map/ppermute | solution.py:247
  32.1 16.8 %collective-permute-start.7 = (bf16[256,256]{1,0:T(8,128)(2,1)}, bf16[256,256]{1,0:T(8,128)(2,1)}, u32[]{:S(2)}, u32[]{:S(2)}) collective-permute-start(bf16[256,256]{1,0:T(8,128)(2,1)} %get-tuple-element.40), channel_id=1, source_target_pairs={{0,18},{2,20},{4,22},{6,24},{8,26},{10,28},{12,30},{14,16},{18,0},... | collective-permute-start | bytes 393224 | tf_op jit(solution)/shard_map/ppermute | solution.py:247
  48.8 16.6 %collective-permute-start.3 = (bf16[256,256]{1,0:T(8,128)(2,1)}, bf16[256,256]{1,0:T(8,128)(2,1)}, u32[]{:S(2)}, u32[]{:S(2)}) collective-permute-start(bf16[256,256]{1,0:T(8,128)(2,1)} %get-tuple-element.36), channel_id=1, source_target_pairs={{0,26},{2,28},{4,30},{6,16},{8,18},{10,20},{12,22},{14,24},{26,0},... | collective-permute-start | bytes 393224 | tf_op jit(solution)/shard_map/ppermute | solution.py:247
  54.4 18.9 %collective-permute-start.1 = (bf16[256,256]{1,0:T(8,128)(2,1)}, bf16[256,256]{1,0:T(8,128)(2,1)}, u32[]{:S(2)}, u32[]{:S(2)}) collective-permute-start(bf16[256,256]{1,0:T(8,128)(2,1)} %get-tuple-element.34), channel_id=1, source_target_pairs={{0,30},{2,16},{4,18},{6,20},{8,22},{10,24},{12,26},{14,28},{30,0},... | collective-permute-start | bytes 393224 | tf_op jit(solution)/shard_map/ppermute | solution.py:247
  58.0 16.9 %collective-permute-start.12 = (bf16[272,256]{1,0:T(8,128)(2,1)}, bf16[272,256]{1,0:T(8,128)(2,1)}, u32[]{:S(2)}, u32[]{:S(2)}) collective-permute-start(bf16[272,256]{1,0:T(8,128)(2,1)} %get-tuple-element.41.refs_5_), channel_id=1, source_target_pairs={{0,16},{2,18},{4,20},{6,22},{8,24},{10,26},{12,28},{14,30},{16,0},... | collective-permute-start | bytes 417800 | tf_op jit(solution)/shard_map/ppermute | solution.py:290
  65.4 16.8 %collective-permute-start.13 = (bf16[272,256]{1,0:T(8,128)(2,1)}, bf16[272,256]{1,0:T(8,128)(2,1)}, u32[]{:S(2)}, u32[]{:S(2)}) collective-permute-start(bf16[272,256]{1,0:T(8,128)(2,1)} %get-tuple-element.47), channel_id=1, source_target_pairs={{0,18},{2,20},{4,22},{6,24},{8,26},{10,28},{12,30},{14,16},{18,0},... | collective-permute-start | bytes 417800 | tf_op jit(solution)/shard_map/ppermute | solution.py:290
  73.3 13.5 %collective-permute-start.10 = (bf16[272,256]{1,0:T(8,128)(2,1)}, bf16[272,256]{1,0:T(8,128)(2,1)}, u32[]{:S(2)}, u32[]{:S(2)}) collective-permute-start(bf16[272,256]{1,0:T(8,128)(2,1)} %get-tuple-element.42.refs_5_), channel_id=1, source_target_pairs={{0,20},{2,22},{4,24},{6,26},{8,28},{10,30},{12,16},{14,18},{20,0},... | collective-permute-start | bytes 417800 | tf_op jit(solution)/shard_map/ppermute | solution.py:290
  74.8 13.5 %collective-permute-start.11 = (bf16[272,256]{1,0:T(8,128)(2,1)}, bf16[272,256]{1,0:T(8,128)(2,1)}, u32[]{:S(2)}, u32[]{:S(2)}) collective-permute-start(bf16[272,256]{1,0:T(8,128)(2,1)} %get-tuple-element.46), channel_id=1, source_target_pairs={{0,22},{2,24},{4,26},{6,28},{8,30},{10,16},{12,18},{14,20},{22,0},... | collective-permute-start | bytes 417800 | tf_op jit(solution)/shard_map/ppermute | solution.py:290
  84.4 6.2 %collective-permute-start.19 = (bf16[2,128,256]{2,1,0:T(8,128)(2,1)}, bf16[2,128,256]{2,1,0:T(8,128)(2,1)}, u32[]{:S(2)}, u32[]{:S(2)}) collective-permute-start(bf16[2,128,256]{2,1,0:T(8,128)(2,1)} %get-tuple-element.52), channel_id=1, source_target_pairs={{0,1},{1,0},{2,3},{3,2},{4,5},{5,4},{6,7},{7,6},{8,9},{9,8},{10,11... | collective-permute-start | bytes 393224 | tf_op jit(solution)/shard_map/ppermute | solution.py:308
  86.8 21.0 %collective-permute-start.17 = (bf16[272,256]{1,0:T(8,128)(2,1)}, bf16[272,256]{1,0:T(8,128)(2,1)}, u32[]{:S(2)}, u32[]{:S(2)}) collective-permute-start(bf16[272,256]{1,0:T(8,128)(2,1)} %get-tuple-element.43.refs_5_), channel_id=1, source_target_pairs={{0,24},{2,26},{4,28},{6,30},{8,16},{10,18},{12,20},{14,22},{24,0},... | collective-permute-start | bytes 417800 | tf_op jit(solution)/shard_map/ppermute | solution.py:290
  88.4 19.5 %collective-permute-start.18 = (bf16[272,256]{1,0:T(8,128)(2,1)}, bf16[272,256]{1,0:T(8,128)(2,1)}, u32[]{:S(2)}, u32[]{:S(2)}) collective-permute-start(bf16[272,256]{1,0:T(8,128)(2,1)} %get-tuple-element.51), channel_id=1, source_target_pairs={{0,26},{2,28},{4,30},{6,16},{8,18},{10,20},{12,22},{14,24},{26,0},... | collective-permute-start | bytes 417800 | tf_op jit(solution)/shard_map/ppermute | solution.py:290
  90.5 19.4 %collective-permute-start.14 = (bf16[2,128,256]{2,1,0:T(8,128)(2,1)}, bf16[2,128,256]{2,1,0:T(8,128)(2,1)}, u32[]{:S(2)}, u32[]{:S(2)}) collective-permute-start(bf16[2,128,256]{2,1,0:T(8,128)(2,1)} %get-tuple-element.50), channel_id=1, source_target_pairs={{0,1},{1,0},{2,3},{3,2},{4,5},{5,4},{6,7},{7,6},{8,9},{9,8},{10,11... | collective-permute-start | bytes 393224 | tf_op jit(solution)/shard_map/ppermute | solution.py:308
  93.9 22.2 %collective-permute-start.8 = (bf16[272,256]{1,0:T(8,128)(2,1)}, bf16[272,256]{1,0:T(8,128)(2,1)}, u32[]{:S(2)}, u32[]{:S(2)}) collective-permute-start(bf16[272,256]{1,0:T(8,128)(2,1)} %get-tuple-element.44.refs_2_), channel_id=1, source_target_pairs={{0,28},{2,30},{4,16},{6,18},{8,20},{10,22},{12,24},{14,26},{28,0},... | collective-permute-start | bytes 417800 | tf_op jit(solution)/shard_map/ppermute | solution.py:290
  101.8 14.3 %collective-permute-start.9 = (bf16[272,256]{1,0:T(8,128)(2,1)}, bf16[272,256]{1,0:T(8,128)(2,1)}, u32[]{:S(2)}, u32[]{:S(2)}) collective-permute-start(bf16[272,256]{1,0:T(8,128)(2,1)} %get-tuple-element.45), channel_id=1, source_target_pairs={{0,30},{2,16},{4,18},{6,20},{8,22},{10,24},{12,26},{14,28},{30,0},... | collective-permute-start | bytes 417800 | tf_op jit(solution)/shard_map/ppermute | solution.py:290
  110.0 10.3 %collective-permute-start.21 = (bf16[2,128,256]{2,1,0:T(8,128)(2,1)}, bf16[2,128,256]{2,1,0:T(8,128)(2,1)}, u32[]{:S(2)}, u32[]{:S(2)}) collective-permute-start(bf16[2,128,256]{2,1,0:T(8,128)(2,1)} %get-tuple-element.56), channel_id=1, source_target_pairs={{0,1},{1,0},{2,3},{3,2},{4,5},{5,4},{6,7},{7,6},{8,9},{9,8},{10,11... | collective-permute-start | bytes 393224 | tf_op jit(solution)/shard_map/ppermute | solution.py:308
  118.2 10.2 %collective-permute-start.20 = (bf16[2,128,256]{2,1,0:T(8,128)(2,1)}, bf16[2,128,256]{2,1,0:T(8,128)(2,1)}, u32[]{:S(2)}, u32[]{:S(2)}) collective-permute-start(bf16[2,128,256]{2,1,0:T(8,128)(2,1)} %get-tuple-element.55), channel_id=1, source_target_pairs={{0,1},{1,0},{2,3},{3,2},{4,5},{5,4},{6,7},{7,6},{8,9},{9,8},{10,11... | collective-permute-start | bytes 393224 | tf_op jit(solution)/shard_map/ppermute | solution.py:308
